TPU v7x, 256 devices: a whole 4x4x8 slice. The times are simulated.
256 devices in a mesh: grp: 8 (over z), feat: 32 (over x, y, core).
Axes of the slice: x: 4, y: 4, z: 8, core: 2. Of those that a mesh axis runs over, the one named last changes fastest.
Arguments:
- features: bfloat16 [65536, 512], P(('grp', 'feat')), may hold values from -6 to 6
- adj_tiles: bfloat16 [512, 16, 128, 128], P(('grp', 'feat')), may hold values from 0.0099487305 to 1
- src_block: int32 [512, 16], P(('grp', 'feat')), may hold values from 0 to 63, as said below
- counts: int32 [512], P(('grp', 'feat')), may hold values from 1 to 16, as said below
- w_self: bfloat16 [512, 512], replicated, may hold values from -0.25 to 0.25
- w_neigh: bfloat16 [512, 512], replicated, may hold values from -0.25 to 0.25
- multiplier: float32 [512], replicated, may hold values from 0.5 to 2
- bit_shift: int32 [512], replicated, may hold values from 0 to 2
- cotangent: bfloat16 [65536, 512], P(('grp', 'feat')), may hold values from -6 to 6
Outputs:
- output: bfloat16 [65536, 512], P(('grp', 'feat'))
- grad_features: bfloat16 [65536, 512], P(('grp', 'feat'))
- grad_self: float32 [512, 512], replicated
- grad_neigh: float32 [512, 512], replicated
Inputs may be any that keep to these rules, and one draw needn't show every extreme that they name: src_block[i, k] is a block of block i's own group, held by a device at most 2 positions from block i's device in the group's cyclic order of devices (block i is held by device (i % 64) // 2 of its group, which holds 2 consecutive blocks); the distance 2 is reached in both directions in every draw. Slots k >= counts[i] take no part.
All inputs are finite; a program needn't handle non-finite values.
Results may differ from a plain program's by a relative error of at most 0.0059.
Values may be sent and summed in bfloat16 or wider, within the bound.
No kernel may reach another device: no remote copies, remote signals or barrier semaphores. Data moves between devices by JAX's collectives and lax.ppermute only.
A program may use at most 64 MiB of HBM per device.

v0:
```python
import math

import jax
import jax.numpy as jnp
from jax import lax
from jax.sharding import PartitionSpec as P

SPAN = 2


def passed_along(x, axis, by):
    peers = lax.axis_size(axis)
    return lax.ppermute(x, axis, [(i, (i + by) % peers) for i in range(peers)])


def fetch_near(shard_piece, steps_by):
    return passed_along(shard_piece, "feat", steps_by)


def return_near(shard_piece, steps_by):
    return passed_along(shard_piece, "feat", steps_by)


def local(
    features, adj_tiles, src_block, counts, w_self, w_neigh, multiplier, bit_shift, cotangent
):
    num_blocks = adj_tiles.shape[0]
    num_slots = adj_tiles.shape[1]
    block_len = adj_tiles.shape[2]
    feature_width = features.shape[1]
    row_count = features.shape[0]
    feat_count = lax.axis_size("feat")
    my_index = lax.axis_index("feat")
    live_mask = jnp.arange(num_slots, dtype=jnp.int32)[None, :] < counts[:, None]
    masked = jnp.where(live_mask[:, :, None, None], adj_tiles, jnp.zeros_like(adj_tiles))
    degree = jnp.sum(masked, axis=(1, 3), dtype=jnp.float32)
    inv_root = lax.rsqrt(degree)
    node_blocks = features.reshape(num_blocks, block_len, feature_width)
    pieces = {0: node_blocks}
    for offset in range(-SPAN, SPAN + 1):
        if offset != 0:
            pieces[offset] = fetch_near(node_blocks, -offset)
    source_pool = jnp.concatenate([pieces[offset] for offset in range(-SPAN, SPAN + 1)], axis=0)
    relative = (src_block // num_blocks - my_index + SPAN) % feat_count
    slot_index = relative * num_blocks + src_block % num_blocks
    flat_index = slot_index.reshape(-1)
    sources = jnp.take(source_pool, flat_index, axis=0).reshape(
        num_blocks, num_slots, block_len, feature_width
    )
    summed = jnp.einsum("bkij,bkjf->bif", masked, sources, preferred_element_type=jnp.float32)
    aggregated = (
        (summed * inv_root[:, :, None]).astype(jnp.bfloat16).reshape(row_count, feature_width)
    )
    preact = jnp.dot(features, w_self, preferred_element_type=jnp.float32)
    preact = preact + jnp.dot(aggregated, w_neigh, preferred_element_type=jnp.float32)
    scale = multiplier * jnp.exp2(-bit_shift.astype(jnp.float32))
    scaled = preact * scale
    sigmoid_val = jax.nn.sigmoid(scaled)
    output = (scaled * sigmoid_val).astype(jnp.bfloat16)
    grad_pre = (
        cotangent.astype(jnp.float32) * sigmoid_val * (1.0 + scaled * (1.0 - sigmoid_val)) * scale
    ).astype(jnp.bfloat16)
    part_self = jnp.dot(features.T, grad_pre, preferred_element_type=jnp.float32)
    part_neigh = jnp.dot(aggregated.T, grad_pre, preferred_element_type=jnp.float32)
    total_self, total_neigh = lax.psum((part_self, part_neigh), ("grp", "feat"))
    grad_scale = 1.0 / math.sqrt(row_count * lax.axis_size("grp") * feat_count)
    own_part = jnp.dot(grad_pre, w_self.T, preferred_element_type=jnp.float32)
    back = jnp.dot(grad_pre, w_neigh.T, preferred_element_type=jnp.float32).reshape(
        num_blocks, block_len, feature_width
    )
    back = (back * inv_root[:, :, None]).astype(jnp.bfloat16)
    contrib = jnp.einsum("bkij,bif->bkjf", masked, back, preferred_element_type=jnp.float32)
    contrib_flat = contrib.reshape(num_blocks * num_slots, block_len * feature_width)
    window_count = (2 * SPAN + 1) * num_blocks
    grouped = jax.ops.segment_sum(contrib_flat, flat_index, num_segments=window_count)
    window = lax.optimization_barrier(grouped.astype(jnp.bfloat16))
    window = window.reshape(window_count, block_len, feature_width)

    def window_piece(offset):
        first_block = (offset + SPAN) * num_blocks
        return window[first_block : first_block + num_blocks]

    spread_blocks = window_piece(0).astype(jnp.float32)
    for offset in range(-SPAN, SPAN + 1):
        if offset != 0:
            arrived = return_near(window_piece(offset), offset)
            spread_blocks = spread_blocks + arrived.astype(jnp.float32)
    spread = spread_blocks.reshape(row_count, feature_width)
    grad_features = (own_part + spread).astype(jnp.bfloat16)
    return (output, grad_features, total_self * grad_scale, total_neigh * grad_scale)


def solution(mesh):
    return jax.shard_map(
        local,
        mesh=mesh,
        in_specs=(
            P(("grp", "feat"), None),
            P(("grp", "feat"), None, None, None),
            P(("grp", "feat"), None),
            P(("grp", "feat")),
            P(),
            P(),
            P(),
            P(),
            P(("grp", "feat"), None),
        ),
        out_specs=(P(("grp", "feat"), None), P(("grp", "feat"), None), P(), P()),
        check_vma=False,
    )
```

profile of v0, /device:TPU:30, one launch (start us, length us, event | category | flops | bytes accessed | tf_op | source)
XLA Modules:
  0.0 400.9 jit_solution(4255000697265647718)
XLA Ops:
  7.2 1.9 collective-permute-start
  9.2 1.7 collective-permute-start.2
  12.6 2.2 fusion.33
  15.5 1.6 convert_reduce_fusion
  17.3 1.1 collective-permute-done.1
  18.5 5.7 %collective-permute-done.3 = bf16[2,128,512]{2,1,0:T(8,128)(2,1)S(1)} collective-permute-done((bf16[2,128,512]{2,1,0:T(8,128)(2,1)}, bf16[2,128,512]{2,1,0:T(8,128)(2,1)S(1)}, u32[]{:S(2)}, u32[]{:S(2)}) %collective-permute-start.3) | collective-permute-done | bytes 262176 | tf_op jit(solution)/shard_map/ppermute | solution.py:13
  24.3 2.8 gather_fusion
  27.0 3.1 fusion.11
  30.2 1.2 multiply_convert_fusion.1
  31.4 1.3 fusion.35
  32.7 1.3 convolution_bitcast_fusion
  34.3 1.4 fusion.14
  35.8 8.1 %copy.21 = f32[4,8,128,512]{3,1,2,0:T(8,128)} copy(f32[4,8,128,512]{3,2,1,0:T(8,128)S(1)} %bitcast.65) | data formatting | bytes 16777216
  43.8 2.2 broadcast_in_dim.35
  46.1 76.2 %scatter_fusion = f32[10,65536]{1,0:T(8,128)} fusion(f32[10,65536]{1,0:T(8,128)} %broadcast_in_dim.35, s32[32]{0:T(128)S(1)} %reshape.113, f32[32,65536]{1,0:T(8,128)} %bitcast.64), kind=kCustom, calls=%fused_computation.1 | custom fusion | flops 2097152 | bytes 25165952 | tf_op jit(solution)/shard_map/scatter-add | solution.py:75
  122.3 2.4 convert_element_type.52
  126.4 5.4 %collective-permute-start.7 = (bf16[2,128,512]{2,1,0:T(8,128)(2,1)S(1)}, bf16[2,128,512]{2,1,0:T(8,128)(2,1)S(1)}, u32[]{:S(2)}, u32[]{:S(2)}) collective-permute-start(bf16[2,128,512]{2,1,0:T(8,128)(2,1)S(1)} %bitcast.81), channel_id=1, source_target_pairs={{0,2},{1,3},{2,4},{3,5},{4,6},{5,7},{6,8},{7,9},{8,10},{9,11},{10,... | collective-permute-start | bytes 786440 | tf_op jit(solution)/shard_map/ppermute | solution.py:13
  131.8 3.5 collective-permute-done.4
  135.3 3.5 collective-permute-done.7
  139.1 1.0 fusion.18
  140.1 249.5 %all-reduce.3.cloned.1.call-done = (f32[512,512]{0,1:T(8,128)}, f32[512,512]{0,1:T(8,128)}) async-done(((f32[512,512]{0,1:T(8,128)}, f32[512,512]{0,1:T(8,128)}), (f32[512,512]{0,1:T(8,128)}, f32[512,512]{0,1:T(8,128)})) %all-reduce.3.cloned.1.call-update) | async-done | bytes 2097168 | tf_op jit(solution)/shard_map/psum | solution.py:65
  389.6 1.8 broadcast_multiply_fusion
  391.4 1.3 copy.15
  392.7 1.3 copy.16
  (43 shorter events, 4.9 us)
Async XLA Ops:
  7.2 23.0 %copy-start = (bf16[512,512]{1,0:T(8,128)(2,1)S(1)}, bf16[512,512]{1,0:T(8,128)(2,1)}, u32[]{:S(2)}) copy-start(bf16[512,512]{1,0:T(8,128)(2,1)} %param.14) | copy-start | bytes 1572868
  7.2 11.2 %copy-start.2 = (bf16[256,512]{1,0:T(8,128)(2,1)S(1)}, bf16[256,512]{1,0:T(8,128)(2,1)}, u32[]{:S(2)}) copy-start(bf16[256,512]{1,0:T(8,128)(2,1)} %param.9) | copy-start | bytes 786436
  7.2 382.4 %all-reduce.3.cloned.1.call-start = ((), (), s32[]{:S(2)}) async-start(), calls=%async_computation | async-start | bytes 4194304 | tf_op jit(solution)/shard_map/psum | solution.py:65
  7.2 10.0 %collective-permute-start = (bf16[2,128,512]{2,1,0:T(8,128)(2,1)}, bf16[2,128,512]{2,1,0:T(8,128)(2,1)S(1)}, u32[]{:S(2)}, u32[]{:S(2)}) collective-permute-start(bf16[2,128,512]{2,1,0:T(8,128)(2,1)} %bitcast.67), channel_id=1, source_target_pairs={{0,2},{1,3},{2,4},{3,5},{4,6},{5,7},{6,8},{7,9},{8,10},{9,11},{10,... | collective-permute-start | bytes 786440 | tf_op jit(solution)/shard_map/ppermute | solution.py:13
  9.2 9.2 %collective-permute-start.1 = (bf16[2,128,512]{2,1,0:T(8,128)(2,1)}, bf16[2,128,512]{2,1,0:T(8,128)(2,1)S(1)}, u32[]{:S(2)}, u32[]{:S(2)}) collective-permute-start(bf16[2,128,512]{2,1,0:T(8,128)(2,1)} %bitcast.68), channel_id=1, source_target_pairs={{0,1},{1,2},{2,3},{3,4},{4,5},{5,6},{6,7},{7,8},{8,9},{9,10},{10,1... | collective-permute-start | bytes 786440 | tf_op jit(solution)/shard_map/ppermute | solution.py:13
  9.2 9.3 %collective-permute-start.2 = (bf16[2,128,512]{2,1,0:T(8,128)(2,1)}, bf16[2,128,512]{2,1,0:T(8,128)(2,1)S(1)}, u32[]{:S(2)}, u32[]{:S(2)}) collective-permute-start(bf16[2,128,512]{2,1,0:T(8,128)(2,1)} %bitcast.69), channel_id=1, source_target_pairs={{0,31},{1,0},{2,1},{3,2},{4,3},{5,4},{6,5},{7,6},{8,7},{9,8},{10,9... | collective-permute-start | bytes 786440 | tf_op jit(solution)/shard_map/ppermute | solution.py:13
  10.9 13.3 %collective-permute-start.3 = (bf16[2,128,512]{2,1,0:T(8,128)(2,1)}, bf16[2,128,512]{2,1,0:T(8,128)(2,1)S(1)}, u32[]{:S(2)}, u32[]{:S(2)}) collective-permute-start(bf16[2,128,512]{2,1,0:T(8,128)(2,1)} %bitcast.70), channel_id=1, source_target_pairs={{0,30},{1,31},{2,0},{3,1},{4,2},{5,3},{6,4},{7,5},{8,6},{9,7},{10,... | collective-permute-start | bytes 786440 | tf_op jit(solution)/shard_map/ppermute | solution.py:13
  24.2 2.8 copy-start.1
  27.0 3.1 copy-start.4
  27.0 3.1 copy-start.5
  125.5 13.5 %copy-start.3 = (bf16[512,512]{1,0:T(8,128)(2,1)S(1)}, bf16[512,512]{1,0:T(8,128)(2,1)}, u32[]{:S(2)}) copy-start(bf16[512,512]{1,0:T(8,128)(2,1)} %param.13) | copy-start | bytes 1572868
  125.6 9.8 %collective-permute-start.4 = (bf16[2,128,512]{2,1,0:T(8,128)(2,1)S(1)}, bf16[2,128,512]{2,1,0:T(8,128)(2,1)S(1)}, u32[]{:S(2)}, u32[]{:S(2)}) collective-permute-start(bf16[2,128,512]{2,1,0:T(8,128)(2,1)S(1)} %bitcast.78), channel_id=1, source_target_pairs={{0,30},{1,31},{2,0},{3,1},{4,2},{5,3},{6,4},{7,5},{8,6},{9,7},{10,... | collective-permute-start | bytes 786440 | tf_op jit(solution)/shard_map/ppermute | solution.py:13
  125.7 9.6 %collective-permute-start.5 = (bf16[2,128,512]{2,1,0:T(8,128)(2,1)S(1)}, bf16[2,128,512]{2,1,0:T(8,128)(2,1)S(1)}, u32[]{:S(2)}, u32[]{:S(2)}) collective-permute-start(bf16[2,128,512]{2,1,0:T(8,128)(2,1)S(1)} %bitcast.79), channel_id=1, source_target_pairs={{0,31},{1,0},{2,1},{3,2},{4,3},{5,4},{6,5},{7,6},{8,7},{9,8},{10,9... | collective-permute-start | bytes 786440 | tf_op jit(solution)/shard_map/ppermute | solution.py:13
  125.8 9.5 %collective-permute-start.6 = (bf16[2,128,512]{2,1,0:T(8,128)(2,1)S(1)}, bf16[2,128,512]{2,1,0:T(8,128)(2,1)S(1)}, u32[]{:S(2)}, u32[]{:S(2)}) collective-permute-start(bf16[2,128,512]{2,1,0:T(8,128)(2,1)S(1)} %bitcast.80), channel_id=1, source_target_pairs={{0,1},{1,2},{2,3},{3,4},{4,5},{5,6},{6,7},{7,8},{8,9},{9,10},{10,1... | collective-permute-start | bytes 786440 | tf_op jit(solution)/shard_map/ppermute | solution.py:13
  126.4 12.5 %collective-permute-start.7 = (bf16[2,128,512]{2,1,0:T(8,128)(2,1)S(1)}, bf16[2,128,512]{2,1,0:T(8,128)(2,1)S(1)}, u32[]{:S(2)}, u32[]{:S(2)}) collective-permute-start(bf16[2,128,512]{2,1,0:T(8,128)(2,1)S(1)} %bitcast.81), channel_id=1, source_target_pairs={{0,2},{1,3},{2,4},{3,5},{4,6},{5,7},{6,8},{7,9},{8,10},{9,11},{10,... | collective-permute-start | bytes 786440 | tf_op jit(solution)/shard_map/ppermute | solution.py:13
Sparse Core Ops, SparseCore 0:
  124.8 264.7 all-reduce.2
where the time goes:
time: 403 us; the launch traced here: 401 us
  waiting for transfers between devices  263 us (65%)
  other arithmetic  85.1 us (21%)
  local copies, waits for them, and re-layouts  16.1 us (4%)
  between operations  14.3 us (4%)
  matrix products  11.9 us (3%)
  starting transfers between devices  10 us (2%)
    psum x1, waiting for transfers between devices, local(): total_self, total_neigh = lax.psum((part_self, part_neigh), ('grp', 'feat'))  250 us
    scatter-add x1, other arithmetic, local(): jax.ops.segment_sum(contrib_flat, flat_index, num_segments=window_count)  76.2 us
    ppermute x8, waiting for transfers between devices, passed_along(): return lax.ppermute(x, axis, [(i, (i + by) % peers) for i in range(peers)])  13.9 us
    unnamed x23, local copies, waits for them, and re-layouts  10.9 us
    ppermute x8, starting transfers between devices, passed_along(): return lax.ppermute(x, axis, [(i, (i + by) % peers) for i in range(peers)])  9.99 us
  transfers between devices with their start and end apart: 9, of which 5 were waited for; matrix products, arithmetic and copies ran while one was open for 2% of the time, Pallas kernels for 0%

commit v1 on v0

v1 whole, which is shorter than its diff:
```python
import math

import jax
import jax.numpy as jnp
from jax import lax
from jax.experimental import pallas as pl
from jax.experimental.pallas import tpu as pltpu
from jax.sharding import Mesh, PartitionSpec as P

SPAN = 2
WINDOW = 2 * SPAN + 1
BF16 = jnp.bfloat16
F32 = jnp.float32
AXES = ("z", "x", "y", "c")
FEAT = ("x", "y", "c")


def passed_along(x, by):
    peers = lax.axis_size(FEAT)
    return lax.ppermute(x, FEAT, [(i, (i + by) % peers) for i in range(peers)])


def to_partner(x):
    return lax.ppermute(x, "c", [(0, 1), (1, 0)])


def dot(a, b):
    return jnp.dot(a, b, preferred_element_type=F32)


def dot_tn(a, b):
    return lax.dot_general(a, b, (((0,), (0,)), ((), ())), preferred_element_type=F32)


def dot_nt(a, b):
    return lax.dot_general(a, b, (((1,), (1,)), ((), ())), preferred_element_type=F32)


def prepare_kernel(peers, where_ref, src_ref, counts_ref, adj_ref, a_ref, at_ref, inv_ref, acc_ref):
    num_blocks, num_slots, block_len, _ = adj_ref.shape
    window_count = acc_ref.shape[0]
    my_index = where_ref[0]
    acc_ref[...] = jnp.zeros(acc_ref.shape, F32)
    for block in range(num_blocks):
        rows = pl.ds(block * block_len, block_len)

        def add_slot(slot, carry, block=block, rows=rows):
            source = src_ref[block, slot]
            relative = lax.rem(source // num_blocks - my_index + SPAN + 2 * peers, peers)
            relative = jnp.minimum(relative, WINDOW - 1)
            place = relative * num_blocks + lax.rem(source, num_blocks)
            acc_ref[place, rows, :] += adj_ref[block, slot].astype(F32)
            return carry

        lax.fori_loop(0, jnp.minimum(counts_ref[block], num_slots), add_slot, 0)
    degree = jnp.zeros(acc_ref.shape[1:], F32)
    for place in range(window_count):
        strip = acc_ref[place]
        degree += strip
        columns = pl.ds(place * block_len, block_len)
        a_ref[:, columns] = strip.astype(BF16)
        at_ref[columns, :] = strip.T.astype(BF16)
    inv_root = lax.rsqrt(jnp.sum(degree, axis=1, keepdims=True))
    inv_ref[...] = jnp.broadcast_to(inv_root, inv_ref.shape)


def forward_kernel(
    core_ref, a_ref, own_ref, m2_ref, m1_ref, p1_ref, p2_ref, inv_ref, ws_ref, wn_ref, scale_ref, cot_ref,
    out_ref, grad_ref, keep_ref, send_ref,
):
    rows = own_ref.shape[0]
    own = own_ref[...]
    summed = jnp.zeros(own.shape, F32)
    for place, ref in enumerate((m2_ref, m1_ref, own_ref, p1_ref, p2_ref)):
        summed += dot(a_ref[:, pl.ds(place * rows, rows)], ref[...])
    aggregated = (summed * inv_ref[:, :1]).astype(BF16)
    preact = dot(own, ws_ref[...]) + dot(aggregated, wn_ref[...])
    scale = scale_ref[...]
    scaled = preact * scale
    sig = jax.nn.sigmoid(scaled)
    out_ref[...] = (scaled * sig).astype(BF16)
    grad = (cot_ref[...].astype(F32) * sig * (1.0 + scaled * (1.0 - sig)) * scale).astype(BF16)
    grad_ref[...] = grad
    first = core_ref[0] == 0
    keep_ref[...] = dot_tn(jnp.where(first, own, aggregated), grad)
    send_ref[...] = dot_tn(jnp.where(first, aggregated, own), grad).astype(BF16)


def backward_kernel(
    grad_ref, at_ref, inv_ref, ws_ref, wn_ref, base_ref, m2_ref, m1_ref, p1_ref, p2_ref
):
    grad = grad_ref[...]
    rows = grad.shape[0]
    back = (dot_nt(grad, wn_ref[...]) * inv_ref[:, :1]).astype(BF16)
    for place, ref in ((0, m2_ref), (1, m1_ref), (3, p1_ref), (4, p2_ref)):
        ref[...] = dot(at_ref[pl.ds(place * rows, rows), :], back).astype(BF16)
    own_term = dot(at_ref[pl.ds(SPAN * rows, rows), :], back).astype(BF16)
    base_ref[...] = dot_nt(grad, ws_ref[...]) + own_term.astype(F32)


def local(
    features, adj_tiles, src_block, counts, w_self, w_neigh, multiplier, bit_shift, cotangent
):
    num_blocks, _, block_len, _ = adj_tiles.shape
    row_count, width = features.shape
    hidden = w_self.shape[1]
    peers = lax.axis_size(FEAT)
    chips = lax.axis_size(("x", "y"))
    groups = lax.axis_size("z")
    my_index = lax.axis_index(FEAT).astype(jnp.int32).reshape(1)
    my_core = lax.axis_index("c").astype(jnp.int32).reshape(1)
    shape = jax.ShapeDtypeStruct
    vmem = pl.BlockSpec(memory_space=pltpu.VMEM)
    smem = pl.BlockSpec(memory_space=pltpu.SMEM)

    near = {by: passed_along(features, -by) for by in (-2, -1, 1, 2)}
    scale = (multiplier * jnp.exp2(-bit_shift.astype(F32))).reshape(1, hidden)
    columns = WINDOW * row_count
    adj, adj_t, inv_root = pl.pallas_call(
        lambda *refs: prepare_kernel(peers, *refs),
        out_shape=(
            shape((row_count, columns), BF16),
            shape((columns, row_count), BF16),
            shape((row_count, 128), F32),
        ),
        in_specs=[smem, smem, smem, vmem],
        out_specs=(vmem, vmem, vmem),
        scratch_shapes=[pltpu.VMEM((WINDOW * num_blocks, row_count, block_len), F32)],
        name="prepare",
    )(my_index, src_block, counts, adj_tiles)

    output, grad_pre, keep, send = pl.pallas_call(
        forward_kernel,
        out_shape=(
            shape((row_count, hidden), BF16),
            shape((row_count, hidden), BF16),
            shape((width, hidden), F32),
            shape((width, hidden), BF16),
        ),
        in_specs=[smem] + [vmem] * 11,
        out_specs=(vmem,) * 4,
        name="forward",
    )(
        my_core, adj, features, near[-2], near[-1], near[1], near[2], inv_root, w_self, w_neigh, scale, cotangent,
    )
    received = to_partner(send)

    base, *terms = pl.pallas_call(
        backward_kernel,
        out_shape=(shape((row_count, width), F32),) + (shape((row_count, width), BF16),) * 4,
        in_specs=[vmem] * 5,
        out_specs=(vmem,) * 5,
        name="backward",
    )(grad_pre, adj_t, inv_root, w_self, w_neigh)
    arrived = [passed_along(term, by) for term, by in zip(terms, (-2, -1, 1, 2))]

    piece_rows = width // chips
    pair = (keep + received.astype(F32)).astype(BF16).reshape(chips, piece_rows, hidden)
    pieces = lax.all_to_all(pair, ("x", "y"), 0, 0)
    plane = jnp.sum(pieces.astype(F32), axis=0).astype(BF16)
    planes = lax.all_to_all(jnp.broadcast_to(plane, (groups,) + plane.shape), "z", 0, 0)
    grad_scale = 1.0 / math.sqrt(row_count * groups * peers)
    total = (jnp.sum(planes.astype(F32), axis=0) * grad_scale).astype(BF16)
    mine = lax.all_to_all(jnp.broadcast_to(total, (chips,) + total.shape), ("x", "y"), 0, 0)
    mine = mine.reshape(width, hidden)
    other = to_partner(mine)
    first = my_core[0] == 0
    grad_self = jnp.where(first, mine, other).astype(F32)
    grad_neigh = jnp.where(first, other, mine).astype(F32)

    spread = base
    for term in arrived:
        spread = spread + term.astype(F32)
    return output, spread.astype(BF16), grad_self, grad_neigh


def solution(mesh):
    feat = mesh.shape["feat"]
    fine = Mesh(mesh.devices.reshape(mesh.shape["grp"], 4, feat // 8, 2), AXES)
    nodes = P(AXES)
    return jax.shard_map(
        local,
        mesh=fine,
        in_specs=(nodes, nodes, nodes, nodes, P(), P(), P(), P(), nodes),
        out_specs=(nodes, nodes, P(), P()),
        check_vma=False,
    )
```

time: 403 us -> 91.4 us (0.23)
  waiting for transfers between devices: 263 us -> 24.9 us
  other arithmetic: 85.1 us -> 5.5 us
  blocking collectives: 0 us -> 32.4 us
  local copies, waits for them, and re-layouts: 16.1 us -> 1.58 us
  between operations: 14.3 us -> 0.68 us
  matrix products: 11.9 us -> 0 us
  Pallas kernels: 0 us -> 10.3 us
  starting transfers between devices: 10 us -> 15.7 us
    psum x1 -> x0, waiting for transfers between devices: 250 us -> none  [local(): total_self, total_neigh = lax.psum((part_self, part_neigh), ('grp', 'feat'))]
    scatter-add x1 -> x0, other arithmetic: 76.2 us -> none  [local(): jax.ops.segment_sum(contrib_flat, flat_index, num_segments=window_count)]
    all_to_all x0 -> x2, blocking collectives: none -> 32.4 us  [the longest x1 18.2 us: local(): lax.all_to_all(jnp.broadcast_to(plane, (groups,) + plane.shape), 'z', 0, 0)]
    dot_general x8 -> x0, matrix products: 11.9 us -> none  [the longest x1 3.1 us: local(): jnp.einsum('bkij,bkjf->bif', masked, sources, preferred_element_type=jnp....]
    ppermute x8 -> x10, waiting for transfers between devices: 13.9 us -> 24.9 us  [the longest x8 22.8 us: passed_along(): return lax.ppermute(x, FEAT, [(i, (i + by) % peers) for i in range(peers)])]
    pallas_call x0 -> x3, Pallas kernels: none -> 10.3 us  [the longest x1 4.35 us: local(): pl.pallas_call(forward_kernel, out_shape=(shape((row_count, hidden), BF16...]
    unnamed x23 -> x12, local copies, waits for them, and re-layouts: 10.9 us -> 0.71 us
    all_to_all x0 -> x1, starting transfers between devices: none -> 8.09 us  [local(): lax.all_to_all(jnp.broadcast_to(total, (chips,) + total.shape), ('x', 'y'...]
  transfers between devices with their start and end apart: 9 -> 11, of which waited for: 5 -> 7; matrix products, arithmetic and copies ran while one was open for 2% -> 3% of each run, Pallas kernels for 0% -> 7%
where the time goes in v1:
time: 91.4 us; the launch traced here: 91 us
  blocking collectives  32.4 us (35%)
  waiting for transfers between devices  24.9 us (27%)
  starting transfers between devices  15.7 us (17%)
  Pallas kernels  10.3 us (11%)
  other arithmetic  5.5 us (6%)
  local copies, waits for them, and re-layouts  1.58 us (2%)
    ppermute x8, waiting for transfers between devices, passed_along(): return lax.ppermute(x, FEAT, [(i, (i + by) % peers) for i in range(peers)])  22.8 us
    all_to_all x1, blocking collectives, local(): lax.all_to_all(jnp.broadcast_to(plane, (groups,) + plane.shape), 'z', 0, 0)  18.2 us
    all_to_all x1, blocking collectives, local(): pieces = lax.all_to_all(pair, ('x', 'y'), 0, 0)  14.1 us
    all_to_all x1, starting transfers between devices, local(): lax.all_to_all(jnp.broadcast_to(total, (chips,) + total.shape), ('x', 'y'...  8.09 us
    ppermute x8, starting transfers between devices, passed_along(): return lax.ppermute(x, FEAT, [(i, (i + by) % peers) for i in range(peers)])  7.62 us
    pallas_call x1, Pallas kernels, local(): pl.pallas_call(forward_kernel, out_shape=(shape((row_count, hidden), BF16...  4.35 us
    pallas_call x1, Pallas kernels, local(): pl.pallas_call(backward_kernel, out_shape=(shape((row_count, width), F32)...  3.26 us
    pallas_call x1, Pallas kernels, local(): pl.pallas_call(lambda *refs: prepare_kernel(peers, *refs), out_shape=(sha...  2.68 us
  transfers between devices with their start and end apart: 11, of which 7 were waited for; matrix products, arithmetic and copies ran while one was open for 3% of the time, Pallas kernels for 7%

profile of v1, /device:TPU:30, one launch (start us, length us, event | category | flops | bytes accessed | tf_op | source)
XLA Modules:
  0.0 91.0 jit_solution(2920212028019558907)
XLA Ops:
  0.6 1.9 %collective-permute-start = (bf16[256,512]{1,0:T(8,128)(2,1)}, bf16[256,512]{1,0:T(8,128)(2,1)S(1)}, u32[]{:S(2)}, u32[]{:S(2)}) collective-permute-start(bf16[256,512]{1,0:T(8,128)(2,1)} %own_ref.1), channel_id=1, source_target_pairs={{0,2},{1,3},{2,4},{3,5},{4,6},{5,7},{6,8},{7,9},{8,10},{9,11},{10,... | collective-permute-start | bytes 786440 | tf_op jit(solution)/shard_map/ppermute | solution.py:20
  2.6 1.7 %collective-permute-start.2 = (bf16[256,512]{1,0:T(8,128)(2,1)}, bf16[256,512]{1,0:T(8,128)(2,1)S(1)}, u32[]{:S(2)}, u32[]{:S(2)}) collective-permute-start(bf16[256,512]{1,0:T(8,128)(2,1)} %own_ref.1), channel_id=1, source_target_pairs={{0,31},{1,0},{2,1},{3,2},{4,3},{5,4},{6,5},{7,6},{8,7},{9,8},{10,9... | collective-permute-start | bytes 786440 | tf_op jit(solution)/shard_map/ppermute | solution.py:20
  4.3 0.2 collective-permute-start.3
  4.5 2.7 %prepare.1 = (bf16[256,1280]{1,0:T(8,128)(2,1)}, bf16[1280,256]{1,0:T(8,128)(2,1)}, f32[256,128]{1,0:T(8,128)}) custom-call(s32[1]{0:T(128)} %bitcast.1.refs_0_, s32[2,16]{1,0:T(2,128)} %refs_1_.1, s32[2]{0:T(128)} %refs_2_.1, bf16[2,16,128,128]{3,2,1,0:T(8,128)(2,1)} %refs_3_.1), custom_call_target="tpu_custom_call" | custom-call | tf_op jit(solution)/shard_map/prepare/pallas_call | solution.py:119
  7.2 0.6 exponential_multiply_fusion
  7.8 2.3 %collective-permute-done.m2_ref = bf16[256,512]{1,0:T(8,128)(2,1)S(1)} collective-permute-done((bf16[256,512]{1,0:T(8,128)(2,1)}, bf16[256,512]{1,0:T(8,128)(2,1)S(1)}, u32[]{:S(2)}, u32[]{:S(2)}) %collective-permute-start) | collective-permute-done | bytes 262176 | tf_op jit(solution)/shard_map/ppermute | solution.py:20
  10.1 1.7 %collective-permute-done.1.m1_ref = bf16[256,512]{1,0:T(8,128)(2,1)S(1)} collective-permute-done((bf16[256,512]{1,0:T(8,128)(2,1)}, bf16[256,512]{1,0:T(8,128)(2,1)S(1)}, u32[]{:S(2)}, u32[]{:S(2)}) %collective-permute-start.1) | collective-permute-done | bytes 262176 | tf_op jit(solution)/shard_map/ppermute | solution.py:20
  11.8 5.8 %collective-permute-done.3.p2_ref = bf16[256,512]{1,0:T(8,128)(2,1)S(1)} collective-permute-done((bf16[256,512]{1,0:T(8,128)(2,1)}, bf16[256,512]{1,0:T(8,128)(2,1)S(1)}, u32[]{:S(2)}, u32[]{:S(2)}) %collective-permute-start.3) | collective-permute-done | bytes 262176 | tf_op jit(solution)/shard_map/ppermute | solution.py:20
  17.6 0.7 copy-done.3
  18.3 4.4 %forward.1 = (bf16[256,512]{1,0:T(8,128)(2,1)}, bf16[256,512]{1,0:T(8,128)(2,1)}, f32[512,512]{1,0:T(8,128)}, bf16[512,512]{1,0:T(8,128)(2,1)}) custom-call(s32[1]{0:T(128)} %bitcast.core_ref, bf16[256,1280]{1,0:T(8,128)(2,1)} %get-tuple-element.16.a_ref, bf16[256,512]{1,0:T(8,128)(2,1)} %own_ref.1, bf16[256,512]{1,0:T(8,128)(2,1)} %copy-done, ...), custom_call_target="tpu_custom_call" | custom-call | tf_op jit(solution)/shard_map/forward/pallas_call | solution.py:132
  22.7 2.1 %collective-permute-done.8 = bf16[512,512]{1,0:T(8,128)(2,1)S(1)} collective-permute-done((bf16[512,512]{1,0:T(8,128)(2,1)}, bf16[512,512]{1,0:T(8,128)(2,1)S(1)}, u32[]{:S(2)}, u32[]{:S(2)}) %collective-permute-start.8) | collective-permute-done | bytes 524320 | tf_op jit(solution)/shard_map/ppermute | solution.py:24
  24.8 1.4 %add_convert_fusion = bf16[512,512]{1,0:T(8,128)(2,1)S(1)} fusion(f32[512,512]{1,0:T(8,128)} %get-tuple-element.26, bf16[512,512]{1,0:T(8,128)(2,1)S(1)} %collective-permute-done.8), kind=kLoop, calls=%fused_computation | loop fusion | flops 786432 | bytes 2097152 | tf_op jit(solution)/shard_map/convert_element_type | solution.py:158
  26.2 14.1 %all_to_all.15 = bf16[16,32,512]{2,1,0:T(8,128)(2,1)S(1)} all-to-all(bf16[16,32,512]{2,1,0:T(8,128)(2,1)S(1)} %bitcast.8), channel_id=1, replica_groups=mesh['z'=8,'x'=4,'y'=4,'c'=2] {'x','y'}, dimensions={0} | all-to-all | bytes 1048576 | tf_op jit(solution)/shard_map/all_to_all | solution.py:159
  40.4 18.2 %all_to_all.16 = bf16[8,32,512]{2,1,0:T(8,128)(2,1)S(1)} all-to-all(bf16[8,32,512]{2,1,0:T(8,128)(2,1)S(1)} %broadcast_in_dim.6), channel_id=1, replica_groups=mesh['z'=8,'x'=4,'y'=4,'c'=2] {'z'}, dimensions={0} | all-to-all | bytes 524288 | tf_op jit(solution)/shard_map/all_to_all | solution.py:161
  58.7 0.8 broadcast_in_dim.7
  59.6 8.1 %all-to-all-start.2 = ((bf16[16,32,512]{2,1,0:T(8,128)(2,1)}), bf16[16,32,512]{2,1,0:T(8,128)(2,1)S(1)}, u32[]{:S(2)}, u32[]{:S(2)}) async-start(bf16[16,32,512]{2,1,0:T(8,128)(2,1)} %broadcast_in_dim.7), calls=%async_computation.2 | async-start | bytes 1048576 | tf_op jit(solution)/shard_map/all_to_all | solution.py:164
  67.6 3.3 %backward.1 = (f32[256,512]{1,0:T(8,128)}, bf16[256,512]{1,0:T(8,128)(2,1)}, bf16[256,512]{1,0:T(8,128)(2,1)}, bf16[256,512]{1,0:T(8,128)(2,1)}, bf16[256,512]{1,0:T(8,128)(2,1)}) custom-call(bf16[256,512]{1,0:T(8,128)(2,1)} %get-tuple-element.19.grad_ref, bf16[1280,256]{1,0:T(8,128)(2,1)} %get-tuple-element.20.at_ref, ...), custom_call_target="tpu_custom_call" | custom-call | tf_op jit(solution)/shard_map/backward/pallas_call | solution.py:148
  71.0 1.7 %collective-permute-start.5 = (bf16[256,512]{1,0:T(8,128)(2,1)}, bf16[256,512]{1,0:T(8,128)(2,1)S(1)}, u32[]{:S(2)}, u32[]{:S(2)}) collective-permute-start(bf16[256,512]{1,0:T(8,128)(2,1)} %get-tuple-element.23), channel_id=1, source_target_pairs={{0,31},{1,0},{2,1},{3,2},{4,3},{5,4},{6,5},{7,6},{8,7},{9,8},{10,9... | collective-permute-start | bytes 786440 | tf_op jit(solution)/shard_map/ppermute | solution.py:20
  72.8 1.9 %collective-permute-start.4 = (bf16[256,512]{1,0:T(8,128)(2,1)}, bf16[256,512]{1,0:T(8,128)(2,1)S(1)}, u32[]{:S(2)}, u32[]{:S(2)}) collective-permute-start(bf16[256,512]{1,0:T(8,128)(2,1)} %get-tuple-element.22), channel_id=1, source_target_pairs={{0,30},{1,31},{2,0},{3,1},{4,2},{5,3},{6,4},{7,5},{8,6},{9,7},{10,... | collective-permute-start | bytes 786440 | tf_op jit(solution)/shard_map/ppermute | solution.py:20
  74.7 5.6 %collective-permute-done.7 = bf16[256,512]{1,0:T(8,128)(2,1)S(1)} collective-permute-done((bf16[256,512]{1,0:T(8,128)(2,1)}, bf16[256,512]{1,0:T(8,128)(2,1)S(1)}, u32[]{:S(2)}, u32[]{:S(2)}) %collective-permute-start.7) | collective-permute-done | bytes 262176 | tf_op jit(solution)/shard_map/ppermute | solution.py:20
  80.3 1.2 %collective-permute-done.6 = bf16[256,512]{1,0:T(8,128)(2,1)S(1)} collective-permute-done((bf16[256,512]{1,0:T(8,128)(2,1)}, bf16[256,512]{1,0:T(8,128)(2,1)S(1)}, u32[]{:S(2)}, u32[]{:S(2)}) %collective-permute-start.6) | collective-permute-done | bytes 262176 | tf_op jit(solution)/shard_map/ppermute | solution.py:20
  81.5 6.1 %collective-permute-done.4 = bf16[256,512]{1,0:T(8,128)(2,1)S(1)} collective-permute-done((bf16[256,512]{1,0:T(8,128)(2,1)}, bf16[256,512]{1,0:T(8,128)(2,1)S(1)}, u32[]{:S(2)}, u32[]{:S(2)}) %collective-permute-start.4) | collective-permute-done | bytes 262176 | tf_op jit(solution)/shard_map/ppermute | solution.py:20
  87.6 1.9 %add_convert_fusion.1 = bf16[256,512]{1,0:T(8,128)(2,1)} fusion(bf16[256,512]{1,0:T(8,128)(2,1)S(1)} %collective-permute-done.7, bf16[256,512]{1,0:T(8,128)(2,1)S(1)} %collective-permute-done.6, bf16[256,512]{1,0:T(8,128)(2,1)S(1)} %collective-permute-done.5, f32[256,512]{1,0:T(8,128)} %get-tuple-element.21, bf16[256,512]{1,0:T(8,128)(2,1)S(1)} %collective-permute-done.4), kind=kLoop, calls=%fused_computation.4 | loop fusion | flops 1179648 | bytes 1835008 | tf_op jit(solution)/shard_map/convert_element_type | solution.py:174
  89.5 1.5 %select_convert_fusion = (f32[512,512]{1,0:T(8,128)}, f32[512,512]{1,0:T(8,128)}) fusion(bf16[512,512]{1,0:T(8,128)(2,1)S(1)} %collective-permute-done.9, pred[]{:T(512)S(6)} %eq.3, bf16[16,32,512]{2,1,0:T(8,128)(2,1)S(1)} %all-to-all-done.2), kind=kLoop, calls=%fused_computation.1 | loop fusion | flops 1048576 | bytes 3145729 | tf_op jit(solution)/shard_map/convert_element_type | solution.py:169
  (24 shorter events, 0.3 us)
Async XLA Ops:
  0.6 9.5 %collective-permute-start = (bf16[256,512]{1,0:T(8,128)(2,1)}, bf16[256,512]{1,0:T(8,128)(2,1)S(1)}, u32[]{:S(2)}, u32[]{:S(2)}) collective-permute-start(bf16[256,512]{1,0:T(8,128)(2,1)} %own_ref.1), channel_id=1, source_target_pairs={{0,2},{1,3},{2,4},{3,5},{4,6},{5,7},{6,8},{7,9},{8,10},{9,11},{10,... | collective-permute-start | bytes 786440 | tf_op jit(solution)/shard_map/ppermute | solution.py:20
  2.6 9.2 %collective-permute-start.1 = (bf16[256,512]{1,0:T(8,128)(2,1)}, bf16[256,512]{1,0:T(8,128)(2,1)S(1)}, u32[]{:S(2)}, u32[]{:S(2)}) collective-permute-start(bf16[256,512]{1,0:T(8,128)(2,1)} %own_ref.1), channel_id=1, source_target_pairs={{0,1},{1,2},{2,3},{3,4},{4,5},{5,6},{6,7},{7,8},{8,9},{9,10},{10,1... | collective-permute-start | bytes 786440 | tf_op jit(solution)/shard_map/ppermute | solution.py:20
  2.6 9.2 %collective-permute-start.2 = (bf16[256,512]{1,0:T(8,128)(2,1)}, bf16[256,512]{1,0:T(8,128)(2,1)S(1)}, u32[]{:S(2)}, u32[]{:S(2)}) collective-permute-start(bf16[256,512]{1,0:T(8,128)(2,1)} %own_ref.1), channel_id=1, source_target_pairs={{0,31},{1,0},{2,1},{3,2},{4,3},{5,4},{6,5},{7,6},{8,7},{9,8},{10,9... | collective-permute-start | bytes 786440 | tf_op jit(solution)/shard_map/ppermute | solution.py:20
  4.3 13.3 %collective-permute-start.3 = (bf16[256,512]{1,0:T(8,128)(2,1)}, bf16[256,512]{1,0:T(8,128)(2,1)S(1)}, u32[]{:S(2)}, u32[]{:S(2)}) collective-permute-start(bf16[256,512]{1,0:T(8,128)(2,1)} %own_ref.1), channel_id=1, source_target_pairs={{0,30},{1,31},{2,0},{3,1},{4,2},{5,3},{6,4},{7,5},{8,6},{9,7},{10,... | collective-permute-start | bytes 786440 | tf_op jit(solution)/shard_map/ppermute | solution.py:20
  4.5 2.7 %copy-start.4 = (f32[512]{0:T(512)S(1)}, f32[512]{0:T(512)}, u32[]{:S(2)}) copy-start(f32[512]{0:T(512)} %param.15) | copy-start | bytes 6148
  4.5 2.7 %copy-start.5 = (s32[512]{0:T(512)S(1)}, s32[512]{0:T(512)}, u32[]{:S(2)}) copy-start(s32[512]{0:T(512)} %param.16) | copy-start | bytes 6148
  10.1 7.5 %copy-start = (bf16[256,512]{1,0:T(8,128)(2,1)}, bf16[256,512]{1,0:T(8,128)(2,1)S(1)}, u32[]{:S(2)}) copy-start(bf16[256,512]{1,0:T(8,128)(2,1)S(1)} %collective-permute-done.m2_ref) | copy-start | bytes 786436
  11.8 5.9 %copy-start.1 = (bf16[256,512]{1,0:T(8,128)(2,1)}, bf16[256,512]{1,0:T(8,128)(2,1)S(1)}, u32[]{:S(2)}) copy-start(bf16[256,512]{1,0:T(8,128)(2,1)S(1)} %collective-permute-done.1.m1_ref) | copy-start | bytes 786436
  11.8 5.8 %copy-start.2 = (bf16[256,512]{1,0:T(8,128)(2,1)}, bf16[256,512]{1,0:T(8,128)(2,1)S(1)}, u32[]{:S(2)}) copy-start(bf16[256,512]{1,0:T(8,128)(2,1)S(1)} %collective-permute-done.2.p1_ref) | copy-start | bytes 786436
  17.6 0.7 copy-start.3
  22.7 2.1 %collective-permute-start.8 = (bf16[512,512]{1,0:T(8,128)(2,1)}, bf16[512,512]{1,0:T(8,128)(2,1)S(1)}, u32[]{:S(2)}, u32[]{:S(2)}) collective-permute-start(bf16[512,512]{1,0:T(8,128)(2,1)} %get-tuple-element.27), channel_id=1, source_target_pairs={{0,1},{1,0},{2,3},{3,2},{4,5},{5,4},{6,7},{7,6},{8,9},{9,8},{10,11... | collective-permute-start | bytes 1572872 | tf_op jit(solution)/shard_map/ppermute | solution.py:24
  59.6 15.1 %all-to-all-start.2 = ((bf16[16,32,512]{2,1,0:T(8,128)(2,1)}), bf16[16,32,512]{2,1,0:T(8,128)(2,1)S(1)}, u32[]{:S(2)}, u32[]{:S(2)}) async-start(bf16[16,32,512]{2,1,0:T(8,128)(2,1)} %broadcast_in_dim.7), calls=%async_computation.2 | async-start | bytes 1048576 | tf_op jit(solution)/shard_map/all_to_all | solution.py:164
  70.9 9.4 %collective-permute-start.7 = (bf16[256,512]{1,0:T(8,128)(2,1)}, bf16[256,512]{1,0:T(8,128)(2,1)S(1)}, u32[]{:S(2)}, u32[]{:S(2)}) collective-permute-start(bf16[256,512]{1,0:T(8,128)(2,1)} %get-tuple-element.25), channel_id=1, source_target_pairs={{0,2},{1,3},{2,4},{3,5},{4,6},{5,7},{6,8},{7,9},{8,10},{9,11},{10,... | collective-permute-start | bytes 786440 | tf_op jit(solution)/shard_map/ppermute | solution.py:20
  71.0 10.5 %collective-permute-start.6 = (bf16[256,512]{1,0:T(8,128)(2,1)}, bf16[256,512]{1,0:T(8,128)(2,1)S(1)}, u32[]{:S(2)}, u32[]{:S(2)}) collective-permute-start(bf16[256,512]{1,0:T(8,128)(2,1)} %get-tuple-element.24), channel_id=1, source_target_pairs={{0,1},{1,2},{2,3},{3,4},{4,5},{5,6},{6,7},{7,8},{8,9},{9,10},{10,1... | collective-permute-start | bytes 786440 | tf_op jit(solution)/shard_map/ppermute | solution.py:20
  71.0 10.5 %collective-permute-start.5 = (bf16[256,512]{1,0:T(8,128)(2,1)}, bf16[256,512]{1,0:T(8,128)(2,1)S(1)}, u32[]{:S(2)}, u32[]{:S(2)}) collective-permute-start(bf16[256,512]{1,0:T(8,128)(2,1)} %get-tuple-element.23), channel_id=1, source_target_pairs={{0,31},{1,0},{2,1},{3,2},{4,3},{5,4},{6,5},{7,6},{8,7},{9,8},{10,9... | collective-permute-start | bytes 786440 | tf_op jit(solution)/shard_map/ppermute | solution.py:20
  72.8 14.9 %collective-permute-start.4 = (bf16[256,512]{1,0:T(8,128)(2,1)}, bf16[256,512]{1,0:T(8,128)(2,1)S(1)}, u32[]{:S(2)}, u32[]{:S(2)}) collective-permute-start(bf16[256,512]{1,0:T(8,128)(2,1)} %get-tuple-element.22), channel_id=1, source_target_pairs={{0,30},{1,31},{2,0},{3,1},{4,2},{5,3},{6,4},{7,5},{8,6},{9,7},{10,... | collective-permute-start | bytes 786440 | tf_op jit(solution)/shard_map/ppermute | solution.py:20
  74.7 14.8 %collective-permute-start.9 = (bf16[512,512]{1,0:T(8,128)(2,1)S(1)}, bf16[512,512]{1,0:T(8,128)(2,1)S(1)}, u32[]{:S(2)}, u32[]{:S(2)}) collective-permute-start(bf16[512,512]{1,0:T(8,128)(2,1)S(1)} %bitcast.7), channel_id=1, source_target_pairs={{0,1},{1,0},{2,3},{3,2},{4,5},{5,4},{6,7},{7,6},{8,9},{9,8},{10,11... | collective-permute-start | bytes 1572872 | tf_op jit(solution)/shard_map/ppermute | solution.py:24

commit v2 on v1

--- a/solution.py
+++ b/solution.py
@@ -7,6 +7,7 @@
 from jax.experimental.pallas import tpu as pltpu
 from jax.sharding import Mesh, PartitionSpec as P
 
+
 SPAN = 2
 WINDOW = 2 * SPAN + 1
 BF16 = jnp.bfloat16
@@ -34,6 +35,28 @@
 
 def dot_nt(a, b):
     return lax.dot_general(a, b, (((1,), (1,)), ((), ())), preferred_element_type=F32)
+
+
+def near(shape, dtype):
+    return pltpu.VMEM(shape, dtype)
+
+
+def far(shape, dtype):
+    return pltpu.HBM(shape, dtype)
+
+
+def call(kernel, scalars, arrays, outs, scratch=()):
+    smem = pl.BlockSpec(memory_space=pltpu.SMEM)
+    vmem = pl.BlockSpec(memory_space=pltpu.VMEM)
+    held = [pltpu.with_memory_space_constraint(a, pltpu.VMEM) for a in arrays]
+    return pl.pallas_call(
+        kernel,
+        out_shape=tuple(outs),
+        in_specs=[smem] * len(scalars) + [vmem] * len(held),
+        out_specs=(vmem,) * len(outs),
+        scratch_shapes=scratch,
+        compiler_params=pltpu.CompilerParams(vmem_limit_bytes=16 * 1024 * 1024),
+    )(*scalars, *held)
 
 
 def prepare_kernel(peers, where_ref, src_ref, counts_ref, adj_ref, a_ref, at_ref, inv_ref, acc_ref):
@@ -98,6 +121,36 @@
     base_ref[...] = dot_nt(grad, ws_ref[...]) + own_term.astype(F32)
 
 
+def pair_kernel(keep_ref, received_ref, pair_ref):
+    pair = keep_ref[...] + received_ref[...].astype(F32)
+    pair_ref[...] = pair.astype(BF16).reshape(pair_ref.shape)
+
+
+def sum_kernel(factor, pieces_ref, copies_ref):
+    total = pieces_ref[0].astype(F32)
+    for piece in range(1, pieces_ref.shape[0]):
+        total += pieces_ref[piece].astype(F32)
+    total = (total * factor).astype(BF16)
+    for copy in range(copies_ref.shape[0]):
+        copies_ref[copy] = total
+
+
+def spread_kernel(base_ref, *refs):
+    *terms, out_ref = refs
+    spread = base_ref[...]
+    for term in terms:
+        spread += term[...].astype(F32)
+    out_ref[...] = spread.astype(BF16)
+
+
+def weights_kernel(core_ref, mine_ref, other_ref, self_ref, neigh_ref):
+    first = core_ref[0] == 0
+    mine = mine_ref[...].reshape(self_ref.shape)
+    other = other_ref[...].reshape(self_ref.shape)
+    self_ref[...] = jnp.where(first, mine, other).astype(F32)
+    neigh_ref[...] = jnp.where(first, other, mine).astype(F32)
+
+
 def local(
     features, adj_tiles, src_block, counts, w_self, w_neigh, multiplier, bit_shift, cotangent
 ):
@@ -109,75 +162,58 @@
     groups = lax.axis_size("z")
     my_index = lax.axis_index(FEAT).astype(jnp.int32).reshape(1)
     my_core = lax.axis_index("c").astype(jnp.int32).reshape(1)
-    shape = jax.ShapeDtypeStruct
-    vmem = pl.BlockSpec(memory_space=pltpu.VMEM)
-    smem = pl.BlockSpec(memory_space=pltpu.SMEM)
-
-    near = {by: passed_along(features, -by) for by in (-2, -1, 1, 2)}
+
+    pulled = [passed_along(features, -by) for by in (-2, -1, 1, 2)]
     scale = (multiplier * jnp.exp2(-bit_shift.astype(F32))).reshape(1, hidden)
     columns = WINDOW * row_count
-    adj, adj_t, inv_root = pl.pallas_call(
+    adj, adj_t, inv_root = call(
         lambda *refs: prepare_kernel(peers, *refs),
-        out_shape=(
-            shape((row_count, columns), BF16),
-            shape((columns, row_count), BF16),
-            shape((row_count, 128), F32),
+        (my_index, src_block, counts),
+        (adj_tiles,),
+        (near((row_count, columns), BF16), near((columns, row_count), BF16), near((row_count, 128), F32)),
+        [pltpu.VMEM((WINDOW * num_blocks, row_count, block_len), F32)],
+    )
+    output, grad_pre, keep, send = call(
+        forward_kernel,
+        (my_core,),
+        (adj, features, *pulled, inv_root, w_self, w_neigh, scale, cotangent),
+        (
+            far((row_count, hidden), BF16),
+            near((row_count, hidden), BF16),
+            near((width, hidden), F32),
+            near((width, hidden), BF16),
         ),
-        in_specs=[smem, smem, smem, vmem],
-        out_specs=(vmem, vmem, vmem),
-        scratch_shapes=[pltpu.VMEM((WINDOW * num_blocks, row_count, block_len), F32)],
-        name="prepare",
-    )(my_index, src_block, counts, adj_tiles)
-
-    output, grad_pre, keep, send = pl.pallas_call(
-        forward_kernel,
-        out_shape=(
-            shape((row_count, hidden), BF16),
-            shape((row_count, hidden), BF16),
-            shape((width, hidden), F32),
-            shape((width, hidden), BF16),
-        ),
-        in_specs=[smem] + [vmem] * 11,
-        out_specs=(vmem,) * 4,
-        name="forward",
-    )(
-        my_core, adj, features, near[-2], near[-1], near[1], near[2], inv_root, w_self, w_neigh, scale, cotangent,
     )
     received = to_partner(send)
-
-    base, *terms = pl.pallas_call(
+    piece_rows = width // chips
+    (pair,) = call(pair_kernel, (), (keep, received), (far((chips, piece_rows, hidden), BF16),))
+    base, *terms = call(
         backward_kernel,
-        out_shape=(shape((row_count, width), F32),) + (shape((row_count, width), BF16),) * 4,
-        in_specs=[vmem] * 5,
-        out_specs=(vmem,) * 5,
-        name="backward",
-    )(grad_pre, adj_t, inv_root, w_self, w_neigh)
+        (),
+        (grad_pre, adj_t, inv_root, w_self, w_neigh),
+        (far((row_count, width), F32),) + (far((row_count, width), BF16),) * 4,
+    )
+
+    pieces = lax.all_to_all(pair, ("x", "y"), 0, 0)
+    (plane,) = call(lambda *refs: sum_kernel(1.0, *refs), (), (pieces,), (far((groups, piece_rows, hidden), BF16),))
     arrived = [passed_along(term, by) for term, by in zip(terms, (-2, -1, 1, 2))]
-
-    piece_rows = width // chips
-    pair = (keep + received.astype(F32)).astype(BF16).reshape(chips, piece_rows, hidden)
-    pieces = lax.all_to_all(pair, ("x", "y"), 0, 0)
-    plane = jnp.sum(pieces.astype(F32), axis=0).astype(BF16)
-    planes = lax.all_to_all(jnp.broadcast_to(plane, (groups,) + plane.shape), "z", 0, 0)
+    planes = lax.all_to_all(plane, "z", 0, 0)
     grad_scale = 1.0 / math.sqrt(row_count * groups * peers)
-    total = (jnp.sum(planes.astype(F32), axis=0) * grad_scale).astype(BF16)
-    mine = lax.all_to_all(jnp.broadcast_to(total, (chips,) + total.shape), ("x", "y"), 0, 0)
-    mine = mine.reshape(width, hidden)
+    (total,) = call(
+        lambda *refs: sum_kernel(grad_scale, *refs), (), (planes,), (far((chips, piece_rows, hidden), BF16),)
+    )
+    mine = lax.all_to_all(total, ("x", "y"), 0, 0)
+    (grad_features,) = call(spread_kernel, (), (base, *arrived), (far((row_count, width), BF16),))
     other = to_partner(mine)
-    first = my_core[0] == 0
-    grad_self = jnp.where(first, mine, other).astype(F32)
-    grad_neigh = jnp.where(first, other, mine).astype(F32)
-
-    spread = base
-    for term in arrived:
-        spread = spread + term.astype(F32)
-    return output, spread.astype(BF16), grad_self, grad_neigh
+    grad_self, grad_neigh = call(weights_kernel, (my_core,), (mine, other), (far((width, hidden), F32),) * 2)
+    return output, grad_features, grad_self, grad_neigh
 
 
 def solution(mesh):
     feat = mesh.shape["feat"]
     fine = Mesh(mesh.devices.reshape(mesh.shape["grp"], 4, feat // 8, 2), AXES)
     nodes = P(AXES)
+
     return jax.shard_map(
         local,
         mesh=fine,

time: 91.4 us -> 100 us (1.094)
  the two profiles are of different devices: /device:TPU:30 before, /device:TPU:1 now
where the time goes in v2:
time: 100 us; the launch traced here: 99.8 us
  blocking collectives  44.6 us (45%)
  waiting for transfers between devices  21.2 us (21%)
  starting transfers between devices  18.7 us (19%)
  Pallas kernels  9.75 us (10%)
  local copies, waits for them, and re-layouts  4.87 us (5%)
    ppermute x8, waiting for transfers between devices, passed_along(): return lax.ppermute(x, FEAT, [(i, (i + by) % peers) for i in range(peers)])  19.3 us
    all_to_all x1, blocking collectives, local(): planes = lax.all_to_all(plane, 'z', 0, 0)  17.6 us
    ppermute x8, starting transfers between devices, passed_along(): return lax.ppermute(x, FEAT, [(i, (i + by) % peers) for i in range(peers)])  14.1 us
    all_to_all x1, blocking collectives, local(): pieces = lax.all_to_all(pair, ('x', 'y'), 0, 0)  14.1 us
    all_to_all x1, blocking collectives, local(): mine = lax.all_to_all(total, ('x', 'y'), 0, 0)  12.9 us
    pallas_call x8, Pallas kernels, call(): pl.pallas_call(kernel, out_shape=tuple(outs), in_specs=[smem] * len(scala...  9.75 us
    unnamed x20, local copies, waits for them, and re-layouts  4.87 us
    ppermute x2, starting transfers between devices, to_partner(): return lax.ppermute(x, 'c', [(0, 1), (1, 0)])  4.6 us
  transfers between devices with their start and end apart: 10, of which 5 were waited for; matrix products, arithmetic and copies ran while one was open for 0% of the time, Pallas kernels for 4%

profile of v2, /device:TPU:1, one launch (start us, length us, event | category | flops | bytes accessed | tf_op | source)
XLA Modules:
  0.0 99.8 jit_solution(514382436908877256)
XLA Ops:
  0.6 3.3 %collective-permute-start.2 = (bf16[256,512]{1,0:T(8,128)(2,1)}, bf16[256,512]{1,0:T(8,128)(2,1)S(1)}, u32[]{:S(2)}, u32[]{:S(2)}) collective-permute-start(bf16[256,512]{1,0:T(8,128)(2,1)} %own_ref.1), channel_id=1, source_target_pairs={{0,31},{1,0},{2,1},{3,2},{4,3},{5,4},{6,5},{7,6},{8,7},{9,8},{10,9... | collective-permute-start | bytes 786440 | tf_op jit(solution)/shard_map/ppermute | solution.py:21
  3.9 0.9 collective-permute-start
  4.8 6.8 %collective-permute-start.3 = (bf16[256,512]{1,0:T(8,128)(2,1)}, bf16[256,512]{1,0:T(8,128)(2,1)S(1)}, u32[]{:S(2)}, u32[]{:S(2)}) collective-permute-start(bf16[256,512]{1,0:T(8,128)(2,1)} %own_ref.1), channel_id=1, source_target_pairs={{0,30},{1,31},{2,0},{3,1},{4,2},{5,3},{6,4},{7,5},{8,6},{9,7},{10,... | collective-permute-start | bytes 786440 | tf_op jit(solution)/shard_map/ppermute | solution.py:21
  12.2 1.2 %copy-done.2 = bf16[2,16,128,128]{3,2,1,0:T(8,128)(2,1)S(1)} copy-done((bf16[2,16,128,128]{3,2,1,0:T(8,128)(2,1)S(1)}, bf16[2,16,128,128]{3,2,1,0:T(8,128)(2,1)}, u32[]{:S(2)}) %copy-start.2) | copy-done | bytes 1048600
  13.5 1.3 %shard_map.120 = (bf16[256,1280]{1,0:T(8,128)(2,1)S(1)}, bf16[1280,256]{1,0:T(8,128)(2,1)S(1)}, f32[256,128]{1,0:T(8,128)S(1)}) custom-call(s32[1]{0:T(128)} %bitcast.1.refs_0_, s32[2,16]{1,0:T(2,128)S(1)} %copy-done.6, s32[2]{0:T(128)S(1)} %copy-done.7, bf16[2,16,128,128]{3,2,1,0:T(8,128)(2,1)S(1)} %copy-done.2), custom_call_target="tpu_custom_call" | custom-call | tf_op jit(solution)/shard_map/pallas_call | solution.py:52
  14.9 6.2 %collective-permute-done.m2_ref = bf16[256,512]{1,0:T(8,128)(2,1)S(1)} collective-permute-done((bf16[256,512]{1,0:T(8,128)(2,1)}, bf16[256,512]{1,0:T(8,128)(2,1)S(1)}, u32[]{:S(2)}, u32[]{:S(2)}) %collective-permute-start) | collective-permute-done | bytes 262176 | tf_op jit(solution)/shard_map/ppermute | solution.py:21
  21.1 0.9 copy-done.4
  22.1 0.9 copy-done.5
  23.0 1.7 %shard_map.121 = (bf16[256,512]{1,0:T(8,128)(2,1)}, bf16[256,512]{1,0:T(8,128)(2,1)S(1)}, f32[512,512]{1,0:T(8,128)S(1)}, bf16[512,512]{1,0:T(8,128)(2,1)S(1)}) custom-call(s32[1]{0:T(128)} %bitcast.core_ref, bf16[256,1280]{1,0:T(8,128)(2,1)S(1)} %get-tuple-element.18.a_ref, bf16[256,512]{1,0:T(8,128)(2,1)S(1)} %copy-done.4, ...), custom_call_target="tpu_custom_call" | custom-call | tf_op jit(solution)/shard_map/pallas_call | solution.py:52
  24.7 1.9 %collective-permute-done.8.received_ref = bf16[512,512]{1,0:T(8,128)(2,1)S(1)} collective-permute-done((bf16[512,512]{1,0:T(8,128)(2,1)S(1)}, bf16[512,512]{1,0:T(8,128)(2,1)S(1)}, u32[]{:S(2)}, u32[]{:S(2)}) %collective-permute-start.8) | collective-permute-done | bytes 524320 | tf_op jit(solution)/shard_map/ppermute | solution.py:25
  26.6 0.9 shard_map.124
  27.5 14.1 %all_to_all.15.refs_0_ = bf16[16,32,512]{2,1,0:T(8,128)(2,1)S(1)} all-to-all(bf16[16,32,512]{2,1,0:T(8,128)(2,1)} %shard_map.124), channel_id=1, replica_groups=mesh['z'=8,'x'=4,'y'=4,'c'=2] {'x','y'}, dimensions={0} | all-to-all | bytes 1048576 | tf_op jit(solution)/shard_map/all_to_all | solution.py:197
  42.4 17.6 %all_to_all.16.refs_0_ = bf16[8,32,512]{2,1,0:T(8,128)(2,1)S(1)} all-to-all(bf16[8,32,512]{2,1,0:T(8,128)(2,1)} %shard_map.125), channel_id=1, replica_groups=mesh['z'=8,'x'=4,'y'=4,'c'=2] {'z'}, dimensions={0} | all-to-all | bytes 524288 | tf_op jit(solution)/shard_map/all_to_all | solution.py:200
  60.0 0.9 shard_map.126
  60.8 12.9 %all_to_all.17.mine_ref = bf16[16,32,512]{2,1,0:T(8,128)(2,1)S(1)} all-to-all(bf16[16,32,512]{2,1,0:T(8,128)(2,1)} %shard_map.126), channel_id=1, replica_groups=mesh['z'=8,'x'=4,'y'=4,'c'=2] {'x','y'}, dimensions={0} | all-to-all | bytes 1048576 | tf_op jit(solution)/shard_map/all_to_all | solution.py:205
  73.7 4.6 %collective-permute-start.9 = (bf16[16,32,512]{2,1,0:T(8,128)(2,1)S(1)}, bf16[16,32,512]{2,1,0:T(8,128)(2,1)S(1)}, u32[]{:S(2)}, u32[]{:S(2)}) collective-permute-start(bf16[16,32,512]{2,1,0:T(8,128)(2,1)S(1)} %all_to_all.17.mine_ref), channel_id=1, source_target_pairs={{0,1},{1,0},{2,3},{3,2},{4,5},{5,4},{6,7},{7,6},{8,9},{9,8},{10,11... | collective-permute-start | bytes 1572872 | tf_op jit(solution)/shard_map/ppermute | solution.py:25
  78.3 2.0 %shard_map.122 = (f32[256,512]{1,0:T(8,128)}, bf16[256,512]{1,0:T(8,128)(2,1)}, bf16[256,512]{1,0:T(8,128)(2,1)}, bf16[256,512]{1,0:T(8,128)(2,1)}, bf16[256,512]{1,0:T(8,128)(2,1)}) custom-call(bf16[256,512]{1,0:T(8,128)(2,1)S(1)} %get-tuple-element.21.grad_ref, bf16[1280,256]{1,0:T(8,128)(2,1)S(1)} %get-tuple-element.22.at_ref, ...), custom_call_target="tpu_custom_call" | custom-call | tf_op jit(solution)/shard_map/pallas_call | solution.py:52
  80.3 0.9 collective-permute-start.4
  81.5 1.5 %collective-permute-start.6 = (bf16[256,512]{1,0:T(8,128)(2,1)}, bf16[256,512]{1,0:T(8,128)(2,1)S(1)}, u32[]{:S(2)}, u32[]{:S(2)}) collective-permute-start(bf16[256,512]{1,0:T(8,128)(2,1)} %get-tuple-element.26), channel_id=1, source_target_pairs={{0,1},{1,2},{2,3},{3,4},{4,5},{5,6},{6,7},{7,8},{8,9},{9,10},{10,1... | collective-permute-start | bytes 786440 | tf_op jit(solution)/shard_map/ppermute | solution.py:21
  83.5 4.9 %collective-permute-done.4.refs_0_ = bf16[256,512]{1,0:T(8,128)(2,1)S(1)} collective-permute-done((bf16[256,512]{1,0:T(8,128)(2,1)}, bf16[256,512]{1,0:T(8,128)(2,1)S(1)}, u32[]{:S(2)}, u32[]{:S(2)}) %collective-permute-start.4) | collective-permute-done | bytes 262176 | tf_op jit(solution)/shard_map/ppermute | solution.py:21
  88.4 3.3 %collective-permute-done.5.refs_1_ = bf16[256,512]{1,0:T(8,128)(2,1)S(1)} collective-permute-done((bf16[256,512]{1,0:T(8,128)(2,1)}, bf16[256,512]{1,0:T(8,128)(2,1)S(1)}, u32[]{:S(2)}, u32[]{:S(2)}) %collective-permute-start.5) | collective-permute-done | bytes 262176 | tf_op jit(solution)/shard_map/ppermute | solution.py:21
  91.6 4.9 %collective-permute-done.7.refs_3_ = bf16[256,512]{1,0:T(8,128)(2,1)S(1)} collective-permute-done((bf16[256,512]{1,0:T(8,128)(2,1)}, bf16[256,512]{1,0:T(8,128)(2,1)S(1)}, u32[]{:S(2)}, u32[]{:S(2)}) %collective-permute-start.7) | collective-permute-done | bytes 262176 | tf_op jit(solution)/shard_map/ppermute | solution.py:21
  96.6 1.0 %copy-done.3 = f32[256,512]{1,0:T(8,128)S(1)} copy-done((f32[256,512]{1,0:T(8,128)S(1)}, f32[256,512]{1,0:T(8,128)}, u32[]{:S(2)}) %copy-start.3) | copy-done | bytes 524312
  98.5 1.4 %shard_map.127 = (f32[512,512]{1,0:T(8,128)}, f32[512,512]{1,0:T(8,128)}) custom-call(s32[1]{0:T(128)} %bitcast.core_ref, bf16[16,32,512]{2,1,0:T(8,128)(2,1)S(1)} %all_to_all.17.mine_ref, bf16[16,32,512]{2,1,0:T(8,128)(2,1)S(1)} %collective-permute-done.9.other_ref), custom_call_target="tpu_custom_call" | custom-call | tf_op jit(solution)/shard_map/pallas_call | solution.py:52
  (28 shorter events, 3.2 us)
Async XLA Ops:
  0.6 14.2 %collective-permute-start.2 = (bf16[256,512]{1,0:T(8,128)(2,1)}, bf16[256,512]{1,0:T(8,128)(2,1)S(1)}, u32[]{:S(2)}, u32[]{:S(2)}) collective-permute-start(bf16[256,512]{1,0:T(8,128)(2,1)} %own_ref.1), channel_id=1, source_target_pairs={{0,31},{1,0},{2,1},{3,2},{4,3},{5,4},{6,5},{7,6},{8,7},{9,8},{10,9... | collective-permute-start | bytes 786440 | tf_op jit(solution)/shard_map/ppermute | solution.py:21
  3.9 10.9 %collective-permute-start.1 = (bf16[256,512]{1,0:T(8,128)(2,1)}, bf16[256,512]{1,0:T(8,128)(2,1)S(1)}, u32[]{:S(2)}, u32[]{:S(2)}) collective-permute-start(bf16[256,512]{1,0:T(8,128)(2,1)} %own_ref.1), channel_id=1, source_target_pairs={{0,1},{1,2},{2,3},{3,4},{4,5},{5,6},{6,7},{7,8},{8,9},{9,10},{10,1... | collective-permute-start | bytes 786440 | tf_op jit(solution)/shard_map/ppermute | solution.py:21
  3.9 17.2 %collective-permute-start = (bf16[256,512]{1,0:T(8,128)(2,1)}, bf16[256,512]{1,0:T(8,128)(2,1)S(1)}, u32[]{:S(2)}, u32[]{:S(2)}) collective-permute-start(bf16[256,512]{1,0:T(8,128)(2,1)} %own_ref.1), channel_id=1, source_target_pairs={{0,2},{1,3},{2,4},{3,5},{4,6},{5,7},{6,8},{7,9},{8,10},{9,11},{10,... | collective-permute-start | bytes 786440 | tf_op jit(solution)/shard_map/ppermute | solution.py:21
  4.8 16.3 %collective-permute-start.3 = (bf16[256,512]{1,0:T(8,128)(2,1)}, bf16[256,512]{1,0:T(8,128)(2,1)S(1)}, u32[]{:S(2)}, u32[]{:S(2)}) collective-permute-start(bf16[256,512]{1,0:T(8,128)(2,1)} %own_ref.1), channel_id=1, source_target_pairs={{0,30},{1,31},{2,0},{3,1},{4,2},{5,3},{6,4},{7,5},{8,6},{9,7},{10,... | collective-permute-start | bytes 786440 | tf_op jit(solution)/shard_map/ppermute | solution.py:21
  11.5 3.3 %copy-start.9 = (s32[512]{0:T(512)S(1)}, s32[512]{0:T(512)}, u32[]{:S(2)}) copy-start(s32[512]{0:T(512)} %param.16) | copy-start | bytes 6148
  11.5 0.7 copy-start.6
  11.5 0.7 copy-start.7
  12.2 1.2 %copy-start.2 = (bf16[2,16,128,128]{3,2,1,0:T(8,128)(2,1)S(1)}, bf16[2,16,128,128]{3,2,1,0:T(8,128)(2,1)}, u32[]{:S(2)}) copy-start(bf16[2,16,128,128]{3,2,1,0:T(8,128)(2,1)} %refs_3_.1) | copy-start | bytes 3145732
  13.5 1.4 %copy-start.8 = (f32[512]{0:T(512)S(1)}, f32[512]{0:T(512)}, u32[]{:S(2)}) copy-start(f32[512]{0:T(512)} %param.15) | copy-start | bytes 6148
  13.5 7.7 %copy-start = (bf16[512,512]{1,0:T(8,128)(2,1)S(1)}, bf16[512,512]{1,0:T(8,128)(2,1)}, u32[]{:S(2)}) copy-start(bf16[512,512]{1,0:T(8,128)(2,1)} %ws_ref.3) | copy-start | bytes 1572868
  13.5 7.7 %copy-start.1 = (bf16[512,512]{1,0:T(8,128)(2,1)S(1)}, bf16[512,512]{1,0:T(8,128)(2,1)}, u32[]{:S(2)}) copy-start(bf16[512,512]{1,0:T(8,128)(2,1)} %wn_ref.3) | copy-start | bytes 1572868
  21.1 1.0 copy-start.4
  22.1 0.9 copy-start.5
  24.7 1.9 %collective-permute-start.8 = (bf16[512,512]{1,0:T(8,128)(2,1)S(1)}, bf16[512,512]{1,0:T(8,128)(2,1)S(1)}, u32[]{:S(2)}, u32[]{:S(2)}) collective-permute-start(bf16[512,512]{1,0:T(8,128)(2,1)S(1)} %get-tuple-element.29), channel_id=1, source_target_pairs={{0,1},{1,0},{2,3},{3,2},{4,5},{5,4},{6,7},{7,6},{8,9},{9,8},{10,11... | collective-permute-start | bytes 1572872 | tf_op jit(solution)/shard_map/ppermute | solution.py:25
  73.7 24.7 %collective-permute-start.9 = (bf16[16,32,512]{2,1,0:T(8,128)(2,1)S(1)}, bf16[16,32,512]{2,1,0:T(8,128)(2,1)S(1)}, u32[]{:S(2)}, u32[]{:S(2)}) collective-permute-start(bf16[16,32,512]{2,1,0:T(8,128)(2,1)S(1)} %all_to_all.17.mine_ref), channel_id=1, source_target_pairs={{0,1},{1,0},{2,3},{3,2},{4,5},{5,4},{6,7},{7,6},{8,9},{9,8},{10,11... | collective-permute-start | bytes 1572872 | tf_op jit(solution)/shard_map/ppermute | solution.py:25
  80.3 8.1 %collective-permute-start.4 = (bf16[256,512]{1,0:T(8,128)(2,1)}, bf16[256,512]{1,0:T(8,128)(2,1)S(1)}, u32[]{:S(2)}, u32[]{:S(2)}) collective-permute-start(bf16[256,512]{1,0:T(8,128)(2,1)} %get-tuple-element.24), channel_id=1, source_target_pairs={{0,30},{1,31},{2,0},{3,1},{4,2},{5,3},{6,4},{7,5},{8,6},{9,7},{10,... | collective-permute-start | bytes 786440 | tf_op jit(solution)/shard_map/ppermute | solution.py:21
  81.2 10.5 %collective-permute-start.5 = (bf16[256,512]{1,0:T(8,128)(2,1)}, bf16[256,512]{1,0:T(8,128)(2,1)S(1)}, u32[]{:S(2)}, u32[]{:S(2)}) collective-permute-start(bf16[256,512]{1,0:T(8,128)(2,1)} %get-tuple-element.25), channel_id=1, source_target_pairs={{0,31},{1,0},{2,1},{3,2},{4,3},{5,4},{6,5},{7,6},{8,7},{9,8},{10,9... | collective-permute-start | bytes 786440 | tf_op jit(solution)/shard_map/ppermute | solution.py:21
  81.5 10.2 %collective-permute-start.6 = (bf16[256,512]{1,0:T(8,128)(2,1)}, bf16[256,512]{1,0:T(8,128)(2,1)S(1)}, u32[]{:S(2)}, u32[]{:S(2)}) collective-permute-start(bf16[256,512]{1,0:T(8,128)(2,1)} %get-tuple-element.26), channel_id=1, source_target_pairs={{0,1},{1,2},{2,3},{3,4},{4,5},{5,6},{6,7},{7,8},{8,9},{9,10},{10,1... | collective-permute-start | bytes 786440 | tf_op jit(solution)/shard_map/ppermute | solution.py:21
  82.9 13.6 %collective-permute-start.7 = (bf16[256,512]{1,0:T(8,128)(2,1)}, bf16[256,512]{1,0:T(8,128)(2,1)S(1)}, u32[]{:S(2)}, u32[]{:S(2)}) collective-permute-start(bf16[256,512]{1,0:T(8,128)(2,1)} %get-tuple-element.27), channel_id=1, source_target_pairs={{0,2},{1,3},{2,4},{3,5},{4,6},{5,7},{6,8},{7,9},{8,10},{9,11},{10,... | collective-permute-start | bytes 786440 | tf_op jit(solution)/shard_map/ppermute | solution.py:21
  96.6 1.0 %copy-start.3 = (f32[256,512]{1,0:T(8,128)S(1)}, f32[256,512]{1,0:T(8,128)}, u32[]{:S(2)}) copy-start(f32[256,512]{1,0:T(8,128)} %get-tuple-element.23.base_ref) | copy-start | bytes 1572868

commit v3 on v2

--- a/solution.py
+++ b/solution.py
@@ -45,24 +45,36 @@
     return pltpu.HBM(shape, dtype)
 
 
-def call(kernel, scalars, arrays, outs, scratch=()):
+def call(kernel, scalars, arrays, outs, scratch=(), remote=(), written=False, aliases=None):
     smem = pl.BlockSpec(memory_space=pltpu.SMEM)
     vmem = pl.BlockSpec(memory_space=pltpu.VMEM)
+    hbm = pl.BlockSpec(memory_space=pltpu.HBM)
     held = [pltpu.with_memory_space_constraint(a, pltpu.VMEM) for a in arrays]
     return pl.pallas_call(
         kernel,
         out_shape=tuple(outs),
-        in_specs=[smem] * len(scalars) + [vmem] * len(held),
-        out_specs=(vmem,) * len(outs),
+        in_specs=[smem] * len(scalars) + [vmem] * len(held) + [hbm] * len(remote),
+        out_specs=(hbm if written else vmem,) * len(outs),
+        input_output_aliases=aliases or {},
         scratch_shapes=scratch,
         compiler_params=pltpu.CompilerParams(vmem_limit_bytes=16 * 1024 * 1024),
-    )(*scalars, *held)
-
-
-def prepare_kernel(peers, where_ref, src_ref, counts_ref, adj_ref, a_ref, at_ref, inv_ref, acc_ref):
+    )(*scalars, *held, *remote)
+
+
+def prepare_kernel(
+    peers, where_ref, src_ref, counts_ref, adj_ref, mult_ref, shift_ref, feat_ref, cot_ref,
+    a_ref, at_ref, inv_ref, own_ref, held_ref, scale_ref, acc_ref, sems,
+):
     num_blocks, num_slots, block_len, _ = adj_ref.shape
     window_count = acc_ref.shape[0]
     my_index = where_ref[0]
+    pulls = [
+        pltpu.make_async_copy(feat_ref, own_ref, sems.at[0]),
+        pltpu.make_async_copy(cot_ref, held_ref, sems.at[1]),
+    ]
+    for pull in pulls:
+        pull.start()
+    scale_ref[...] = mult_ref[...] / jnp.left_shift(1, shift_ref[...]).astype(F32)
     acc_ref[...] = jnp.zeros(acc_ref.shape, F32)
     for block in range(num_blocks):
         rows = pl.ds(block * block_len, block_len)
@@ -85,34 +97,43 @@
         at_ref[columns, :] = strip.T.astype(BF16)
     inv_root = lax.rsqrt(jnp.sum(degree, axis=1, keepdims=True))
     inv_ref[...] = jnp.broadcast_to(inv_root, inv_ref.shape)
+    for pull in pulls:
+        pull.wait()
 
 
 def forward_kernel(
-    core_ref, a_ref, own_ref, m2_ref, m1_ref, p1_ref, p2_ref, inv_ref, ws_ref, wn_ref, scale_ref, cot_ref,
-    out_ref, grad_ref, keep_ref, send_ref,
+    core_ref, a_ref, own_ref, m2_ref, p2_ref, partner_ref, m1_ref, p1_ref, inv_ref, ws_ref, wn_ref, scale_ref,
+    cot_ref, out_ref, mine_ref,
 ):
     rows = own_ref.shape[0]
+    first = core_ref[0] == 0
     own = own_ref[...]
+    partner = partner_ref[...]
+    blocks = (
+        m2_ref[...],
+        jnp.where(first, m1_ref[...], partner),
+        own,
+        jnp.where(first, partner, p1_ref[...]),
+        p2_ref[...],
+    )
     summed = jnp.zeros(own.shape, F32)
-    for place, ref in enumerate((m2_ref, m1_ref, own_ref, p1_ref, p2_ref)):
-        summed += dot(a_ref[:, pl.ds(place * rows, rows)], ref[...])
+    for place, block in enumerate(blocks):
+        summed += dot(a_ref[:, pl.ds(place * rows, rows)], block)
     aggregated = (summed * inv_ref[:, :1]).astype(BF16)
+    mine_ref[1] = aggregated
     preact = dot(own, ws_ref[...]) + dot(aggregated, wn_ref[...])
     scale = scale_ref[...]
     scaled = preact * scale
     sig = jax.nn.sigmoid(scaled)
     out_ref[...] = (scaled * sig).astype(BF16)
-    grad = (cot_ref[...].astype(F32) * sig * (1.0 + scaled * (1.0 - sig)) * scale).astype(BF16)
-    grad_ref[...] = grad
-    first = core_ref[0] == 0
-    keep_ref[...] = dot_tn(jnp.where(first, own, aggregated), grad)
-    send_ref[...] = dot_tn(jnp.where(first, aggregated, own), grad).astype(BF16)
+    grad = cot_ref[...].astype(F32) * sig * (1.0 + scaled * (1.0 - sig)) * scale
+    mine_ref[0] = grad.astype(BF16)
 
 
 def backward_kernel(
-    grad_ref, at_ref, inv_ref, ws_ref, wn_ref, base_ref, m2_ref, m1_ref, p1_ref, p2_ref
-):
-    grad = grad_ref[...]
+    mine_ref, at_ref, inv_ref, ws_ref, wn_ref, base_ref, m2_ref, m1_ref, p1_ref, p2_ref
+):
+    grad = mine_ref[0]
     rows = grad.shape[0]
     back = (dot_nt(grad, wn_ref[...]) * inv_ref[:, :1]).astype(BF16)
     for place, ref in ((0, m2_ref), (1, m1_ref), (3, p1_ref), (4, p2_ref)):
@@ -121,8 +142,10 @@
     base_ref[...] = dot_nt(grad, ws_ref[...]) + own_term.astype(F32)
 
 
-def pair_kernel(keep_ref, received_ref, pair_ref):
-    pair = keep_ref[...] + received_ref[...].astype(F32)
+def pair_kernel(core_ref, own_ref, partner_ref, mine_ref, theirs_ref, pair_ref):
+    first = core_ref[0] == 0
+    pair = dot_tn(jnp.where(first, own_ref[...], mine_ref[1]), mine_ref[0])
+    pair += dot_tn(jnp.where(first, partner_ref[...], theirs_ref[1]), theirs_ref[0])
     pair_ref[...] = pair.astype(BF16).reshape(pair_ref.shape)
 
 
@@ -143,12 +166,34 @@
     out_ref[...] = spread.astype(BF16)
 
 
-def weights_kernel(core_ref, mine_ref, other_ref, self_ref, neigh_ref):
-    first = core_ref[0] == 0
-    mine = mine_ref[...].reshape(self_ref.shape)
-    other = other_ref[...].reshape(self_ref.shape)
-    self_ref[...] = jnp.where(first, mine, other).astype(F32)
-    neigh_ref[...] = jnp.where(first, other, mine).astype(F32)
+def widen(to_self, matrix_ref, self_ref, neigh_ref, wide_ref, sems):
+    parts = sems.shape[0]
+    pieces = matrix_ref.shape[0] // parts
+    rows = wide_ref.shape[0] // parts
+    for part in range(parts):
+        here = pl.ds(part * rows, rows)
+        matrix = matrix_ref[pl.ds(part * pieces, pieces)]
+        wide_ref[here, :] = matrix.reshape(rows, wide_ref.shape[1]).astype(F32)
+
+        @pl.when(to_self)
+        def _(part=part, here=here):
+            pltpu.make_async_copy(wide_ref.at[here], self_ref.at[here], sems.at[part]).start()
+
+        @pl.when(jnp.logical_not(to_self))
+        def _(part=part, here=here):
+            pltpu.make_async_copy(wide_ref.at[here], neigh_ref.at[here], sems.at[part]).start()
+
+    for part in range(parts):
+        here = pl.ds(part * rows, rows)
+        pltpu.make_async_copy(wide_ref.at[here], self_ref.at[here], sems.at[part]).wait()
+
+
+def write_mine_kernel(core_ref, matrix_ref, self_ref, neigh_ref, wide_ref, sems):
+    widen(core_ref[0] == 0, matrix_ref, self_ref, neigh_ref, wide_ref, sems)
+
+
+def write_other_kernel(core_ref, matrix_ref, self_in, neigh_in, self_ref, neigh_ref, wide_ref, sems):
+    widen(core_ref[0] != 0, matrix_ref, self_ref, neigh_ref, wide_ref, sems)
 
 
 def local(
@@ -163,34 +208,41 @@
     my_index = lax.axis_index(FEAT).astype(jnp.int32).reshape(1)
     my_core = lax.axis_index("c").astype(jnp.int32).reshape(1)
 
-    pulled = [passed_along(features, -by) for by in (-2, -1, 1, 2)]
-    scale = (multiplier * jnp.exp2(-bit_shift.astype(F32))).reshape(1, hidden)
+    m2 = passed_along(features, 2)
+    p2 = passed_along(features, -2)
+    partner = to_partner(features)
+    m1 = to_partner(m2)
+    p1 = to_partner(p2)
     columns = WINDOW * row_count
-    adj, adj_t, inv_root = call(
+    rows = (row_count, width)
+    adj, adj_t, inv_root, own, held, scale = call(
         lambda *refs: prepare_kernel(peers, *refs),
         (my_index, src_block, counts),
-        (adj_tiles,),
-        (near((row_count, columns), BF16), near((columns, row_count), BF16), near((row_count, 128), F32)),
-        [pltpu.VMEM((WINDOW * num_blocks, row_count, block_len), F32)],
-    )
-    output, grad_pre, keep, send = call(
+        (adj_tiles, multiplier.reshape(1, -1), bit_shift.reshape(1, -1)),
+        (
+            near((row_count, columns), BF16),
+            near((columns, row_count), BF16),
+            near((row_count, 128), F32),
+            near(rows, BF16),
+            near((row_count, hidden), BF16),
+            near((1, hidden), F32),
+        ),
+        [pltpu.VMEM((WINDOW * num_blocks, row_count, block_len), F32), pltpu.SemaphoreType.DMA((2,))],
+        remote=(features, cotangent),
+    )
+    output, mine = call(
         forward_kernel,
         (my_core,),
-        (adj, features, *pulled, inv_root, w_self, w_neigh, scale, cotangent),
-        (
-            far((row_count, hidden), BF16),
-            near((row_count, hidden), BF16),
-            near((width, hidden), F32),
-            near((width, hidden), BF16),
-        ),
-    )
-    received = to_partner(send)
+        (adj, own, m2, p2, partner, m1, p1, inv_root, w_self, w_neigh, scale, held),
+        (far((row_count, hidden), BF16), near((2, row_count, hidden), BF16)),
+    )
+    theirs = to_partner(mine)
     piece_rows = width // chips
-    (pair,) = call(pair_kernel, (), (keep, received), (far((chips, piece_rows, hidden), BF16),))
+    (pair,) = call(pair_kernel, (my_core,), (own, partner, mine, theirs), (far((chips, piece_rows, hidden), BF16),))
     base, *terms = call(
         backward_kernel,
         (),
-        (grad_pre, adj_t, inv_root, w_self, w_neigh),
+        (mine, adj_t, inv_root, w_self, w_neigh),
         (far((row_count, width), F32),) + (far((row_count, width), BF16),) * 4,
     )
 
@@ -202,10 +254,15 @@
     (total,) = call(
         lambda *refs: sum_kernel(grad_scale, *refs), (), (planes,), (far((chips, piece_rows, hidden), BF16),)
     )
-    mine = lax.all_to_all(total, ("x", "y"), 0, 0)
+    matrix = lax.all_to_all(total, ("x", "y"), 0, 0)
     (grad_features,) = call(spread_kernel, (), (base, *arrived), (far((row_count, width), BF16),))
-    other = to_partner(mine)
-    grad_self, grad_neigh = call(weights_kernel, (my_core,), (mine, other), (far((width, hidden), F32),) * 2)
+    other = to_partner(matrix)
+    outs = (far((width, hidden), F32),) * 2
+    scratch = [pltpu.VMEM((width, hidden), F32), pltpu.SemaphoreType.DMA((4,))]
+    written = call(write_mine_kernel, (my_core,), (matrix,), outs, scratch, written=True)
+    grad_self, grad_neigh = call(
+        write_other_kernel, (my_core,), (other,), outs, scratch, remote=written, written=True, aliases={2: 0, 3: 1}
+    )
     return output, grad_features, grad_self, grad_neigh
 
 

time: 100 us -> 100 us (level)
  waiting for transfers between devices: 21.2 us -> 16.3 us
  blocking collectives: 44.6 us -> 47.7 us
  Pallas kernels: 9.75 us -> 10.8 us
    ppermute x2 -> x5, starting transfers between devices: 4.6 us -> 10.2 us  [to_partner(): return lax.ppermute(x, 'c', [(0, 1), (1, 0)])]
    ppermute x8 -> x6, starting transfers between devices: 14.1 us -> 9.13 us  [passed_along(): return lax.ppermute(x, FEAT, [(i, (i + by) % peers) for i in range(peers)])]
    ppermute x8 -> x6, waiting for transfers between devices: 19.3 us -> 14.6 us  [passed_along(): return lax.ppermute(x, FEAT, [(i, (i + by) % peers) for i in range(peers)])]
    all_to_all x1, blocking collectives: 14.1 us -> 16.6 us  [local(): pieces = lax.all_to_all(pair, ('x', 'y'), 0, 0)]
    pallas_call x8 -> x9, Pallas kernels: 9.75 us -> 10.8 us  [call(): pl.pallas_call(kernel, out_shape=tuple(outs), in_specs=[smem] * len(scala...]
  transfers between devices with their start and end apart: 10 -> 11, of which waited for: 5 -> 5; matrix products, arithmetic and copies ran while one was open for 0% -> 0% of each run, Pallas kernels for 4% -> 5%
where the time goes in v3:
time: 100 us; the launch traced here: 99.8 us
  blocking collectives  47.7 us (48%)
  starting transfers between devices  19.3 us (19%)
  waiting for transfers between devices  16.3 us (16%)
  Pallas kernels  10.8 us (11%)
  local copies, waits for them, and re-layouts  4.86 us (5%)
    all_to_all x1, blocking collectives, local(): planes = lax.all_to_all(plane, 'z', 0, 0)  17.3 us
    all_to_all x1, blocking collectives, local(): pieces = lax.all_to_all(pair, ('x', 'y'), 0, 0)  16.6 us
    ppermute x6, waiting for transfers between devices, passed_along(): return lax.ppermute(x, FEAT, [(i, (i + by) % peers) for i in range(peers)])  14.6 us
    all_to_all x1, blocking collectives, local(): matrix = lax.all_to_all(total, ('x', 'y'), 0, 0)  13.8 us
    pallas_call x9, Pallas kernels, call(): pl.pallas_call(kernel, out_shape=tuple(outs), in_specs=[smem] * len(scala...  10.8 us
    ppermute x5, starting transfers between devices, to_partner(): return lax.ppermute(x, 'c', [(0, 1), (1, 0)])  10.2 us
    ppermute x6, starting transfers between devices, passed_along(): return lax.ppermute(x, FEAT, [(i, (i + by) % peers) for i in range(peers)])  9.13 us
    unnamed x20, local copies, waits for them, and re-layouts  4.86 us
  transfers between devices with their start and end apart: 11, of which 5 were waited for; matrix products, arithmetic and copies ran while one was open for 0% of the time, Pallas kernels for 5%

profile of v3, /device:TPU:1, one launch (start us, length us, event | category | flops | bytes accessed | tf_op | source)
XLA Modules:
  0.0 99.8 jit_solution(15513423419736171751)
XLA Ops:
  0.6 2.2 %collective-permute-start = (bf16[256,512]{1,0:T(8,128)(2,1)}, bf16[256,512]{1,0:T(8,128)(2,1)S(1)}, u32[]{:S(2)}, u32[]{:S(2)}) collective-permute-start(bf16[256,512]{1,0:T(8,128)(2,1)} %refs_6_.1), channel_id=1, source_target_pairs={{0,2},{1,3},{2,4},{3,5},{4,6},{5,7},{6,8},{7,9},{8,10},{9,11},{10,... | collective-permute-start | bytes 786440 | tf_op jit(solution)/shard_map/ppermute | solution.py:21
  2.8 3.7 %collective-permute-start.1 = (bf16[256,512]{1,0:T(8,128)(2,1)}, bf16[256,512]{1,0:T(8,128)(2,1)S(1)}, u32[]{:S(2)}, u32[]{:S(2)}) collective-permute-start(bf16[256,512]{1,0:T(8,128)(2,1)} %refs_6_.1), channel_id=1, source_target_pairs={{0,30},{1,31},{2,0},{3,1},{4,2},{5,3},{6,4},{7,5},{8,6},{9,7},{10,... | collective-permute-start | bytes 786440 | tf_op jit(solution)/shard_map/ppermute | solution.py:21
  6.5 2.7 %collective-permute-start.2 = (bf16[256,512]{1,0:T(8,128)(2,1)}, bf16[256,512]{1,0:T(8,128)(2,1)S(1)}, u32[]{:S(2)}, u32[]{:S(2)}) collective-permute-start(bf16[256,512]{1,0:T(8,128)(2,1)} %refs_6_.1), channel_id=1, source_target_pairs={{0,1},{1,0},{2,3},{3,2},{4,5},{5,4},{6,7},{7,6},{8,9},{9,8},{10,11... | collective-permute-start | bytes 786440 | tf_op jit(solution)/shard_map/ppermute | solution.py:25
  9.3 1.6 %collective-permute-done.m2_ref = bf16[256,512]{1,0:T(8,128)(2,1)S(1)} collective-permute-done((bf16[256,512]{1,0:T(8,128)(2,1)}, bf16[256,512]{1,0:T(8,128)(2,1)S(1)}, u32[]{:S(2)}, u32[]{:S(2)}) %collective-permute-start) | collective-permute-done | bytes 262176 | tf_op jit(solution)/shard_map/ppermute | solution.py:21
  10.8 3.1 %collective-permute-start.3 = (bf16[256,512]{1,0:T(8,128)(2,1)S(1)}, bf16[256,512]{1,0:T(8,128)(2,1)S(1)}, u32[]{:S(2)}, u32[]{:S(2)}) collective-permute-start(bf16[256,512]{1,0:T(8,128)(2,1)S(1)} %collective-permute-done.m2_ref), channel_id=1, source_target_pairs={{0,1},{1,0},{2,3},{3,2},{4,5},{5,4},{6,7},{7,6},{8,9},{9,8},{10,11... | collective-permute-start | bytes 786440 | tf_op jit(solution)/shard_map/ppermute | solution.py:25
  14.7 1.2 %copy-done.2 = bf16[2,16,128,128]{3,2,1,0:T(8,128)(2,1)S(1)} copy-done((bf16[2,16,128,128]{3,2,1,0:T(8,128)(2,1)S(1)}, bf16[2,16,128,128]{3,2,1,0:T(8,128)(2,1)}, u32[]{:S(2)}) %copy-start.2) | copy-done | bytes 1048600
  15.9 0.9 copy-done.4
  16.8 0.9 copy-done.5
  17.8 1.4 %shard_map.120 = (bf16[256,1280]{1,0:T(8,128)(2,1)S(1)}, bf16[1280,256]{1,0:T(8,128)(2,1)S(1)}, f32[256,128]{1,0:T(8,128)S(1)}, bf16[256,512]{1,0:T(8,128)(2,1)S...) custom-call(s32[1]{0:T(128)} %bitcast.1.refs_0_, s32[2,16]{1,0:T(2,128)S(1)} %copy-done.8, s32[2]{0:T(128)S(1)} %copy-done.9, ...), custom_call_target="tpu_custom_call" | custom-call | tf_op jit(solution)/shard_map/pallas_call | solution.py:53
  19.2 1.7 %shard_map.121 = (bf16[256,512]{1,0:T(8,128)(2,1)}, bf16[2,256,512]{2,1,0:T(8,128)(2,1)S(1)}) custom-call(s32[1]{0:T(128)} %bitcast.core_ref, bf16[256,1280]{1,0:T(8,128)(2,1)S(1)} %get-tuple-element.21.a_ref, bf16[256,512]{1,0:T(8,128)(2,1)S(1)} %get-tuple-element.22.own_ref, bf16[256,512]{1,0:T(8,128)(2,1)S(1)} %collective-permute-done.m2_ref, ...), custom_call_target="tpu_custom_call" | custom-call | tf_op jit(solution)/shard_map/pallas_call | solution.py:53
  21.2 1.6 %collective-permute-done.9.theirs_ref = bf16[2,256,512]{2,1,0:T(8,128)(2,1)S(1)} collective-permute-done((bf16[2,256,512]{2,1,0:T(8,128)(2,1)S(1)}, bf16[2,256,512]{2,1,0:T(8,128)(2,1)S(1)}, u32[]{:S(2)}, u32[]{:S(2)}) %collective-permute-start.9) | collective-permute-done | bytes 524320 | tf_op jit(solution)/shard_map/ppermute | solution.py:25
  22.9 1.3 %shard_map.124 = bf16[16,32,512]{2,1,0:T(8,128)(2,1)} custom-call(s32[1]{0:T(128)} %bitcast.core_ref, bf16[256,512]{1,0:T(8,128)(2,1)S(1)} %get-tuple-element.22.own_ref, bf16[256,512]{1,0:T(8,128)(2,1)S(1)} %collective-permute-done.2.partner_ref, bf16[2,256,512]{2,1,0:T(8,128)(2,1)S(1)} %get-tuple-element.27.mine_ref, ...), custom_call_target="tpu_custom_call" | custom-call | tf_op jit(solution)/shard_map/pallas_call | solution.py:53
  24.1 16.6 %all_to_all.15.refs_0_ = bf16[16,32,512]{2,1,0:T(8,128)(2,1)S(1)} all-to-all(bf16[16,32,512]{2,1,0:T(8,128)(2,1)} %shard_map.124), channel_id=1, replica_groups=mesh['z'=8,'x'=4,'y'=4,'c'=2] {'x','y'}, dimensions={0} | all-to-all | bytes 1048576 | tf_op jit(solution)/shard_map/all_to_all | solution.py:249
  41.5 17.3 %all_to_all.16.refs_0_ = bf16[8,32,512]{2,1,0:T(8,128)(2,1)S(1)} all-to-all(bf16[8,32,512]{2,1,0:T(8,128)(2,1)} %shard_map.125), channel_id=1, replica_groups=mesh['z'=8,'x'=4,'y'=4,'c'=2] {'z'}, dimensions={0} | all-to-all | bytes 524288 | tf_op jit(solution)/shard_map/all_to_all | solution.py:252
  59.6 13.8 %all_to_all.17.matrix_ref = bf16[16,32,512]{2,1,0:T(8,128)(2,1)S(1)} all-to-all(bf16[16,32,512]{2,1,0:T(8,128)(2,1)} %shard_map.126), channel_id=1, replica_groups=mesh['z'=8,'x'=4,'y'=4,'c'=2] {'x','y'}, dimensions={0} | all-to-all | bytes 1048576 | tf_op jit(solution)/shard_map/all_to_all | solution.py:257
  73.5 4.1 %collective-permute-start.10 = (bf16[16,32,512]{2,1,0:T(8,128)(2,1)S(1)}, bf16[16,32,512]{2,1,0:T(8,128)(2,1)S(1)}, u32[]{:S(2)}, u32[]{:S(2)}) collective-permute-start(bf16[16,32,512]{2,1,0:T(8,128)(2,1)S(1)} %all_to_all.17.matrix_ref), channel_id=1, source_target_pairs={{0,1},{1,0},{2,3},{3,2},{4,5},{5,4},{6,7},{7,6},{8,9},{9,8},{10,11... | collective-permute-start | bytes 1572872 | tf_op jit(solution)/shard_map/ppermute | solution.py:25
  77.6 1.9 %shard_map.122 = (f32[256,512]{1,0:T(8,128)}, bf16[256,512]{1,0:T(8,128)(2,1)}, bf16[256,512]{1,0:T(8,128)(2,1)}, bf16[256,512]{1,0:T(8,128)(2,1)}, bf16[256,512]{1,0:T(8,128)(2,1)}) custom-call(bf16[2,256,512]{2,1,0:T(8,128)(2,1)S(1)} %get-tuple-element.27.mine_ref, bf16[1280,256]{1,0:T(8,128)(2,1)S(1)} %get-tuple-element.28.at_ref, ...), custom_call_target="tpu_custom_call" | custom-call | tf_op jit(solution)/shard_map/pallas_call | solution.py:53
  80.7 1.5 %collective-permute-start.7 = (bf16[256,512]{1,0:T(8,128)(2,1)}, bf16[256,512]{1,0:T(8,128)(2,1)S(1)}, u32[]{:S(2)}, u32[]{:S(2)}) collective-permute-start(bf16[256,512]{1,0:T(8,128)(2,1)} %get-tuple-element.32), channel_id=1, source_target_pairs={{0,1},{1,2},{2,3},{3,4},{4,5},{5,6},{6,7},{7,8},{8,9},{9,10},{10,1... | collective-permute-start | bytes 786440 | tf_op jit(solution)/shard_map/ppermute | solution.py:21
  82.8 4.9 %collective-permute-done.5.refs_0_ = bf16[256,512]{1,0:T(8,128)(2,1)S(1)} collective-permute-done((bf16[256,512]{1,0:T(8,128)(2,1)}, bf16[256,512]{1,0:T(8,128)(2,1)S(1)}, u32[]{:S(2)}, u32[]{:S(2)}) %collective-permute-start.5) | collective-permute-done | bytes 262176 | tf_op jit(solution)/shard_map/ppermute | solution.py:21
  87.6 3.3 %collective-permute-done.6.refs_1_ = bf16[256,512]{1,0:T(8,128)(2,1)S(1)} collective-permute-done((bf16[256,512]{1,0:T(8,128)(2,1)}, bf16[256,512]{1,0:T(8,128)(2,1)S(1)}, u32[]{:S(2)}, u32[]{:S(2)}) %collective-permute-start.6) | collective-permute-done | bytes 262176 | tf_op jit(solution)/shard_map/ppermute | solution.py:21
  90.9 4.9 %collective-permute-done.8.refs_3_ = bf16[256,512]{1,0:T(8,128)(2,1)S(1)} collective-permute-done((bf16[256,512]{1,0:T(8,128)(2,1)}, bf16[256,512]{1,0:T(8,128)(2,1)S(1)}, u32[]{:S(2)}, u32[]{:S(2)}) %collective-permute-start.8) | collective-permute-done | bytes 262176 | tf_op jit(solution)/shard_map/ppermute | solution.py:21
  95.8 1.0 %copy-done.3 = f32[256,512]{1,0:T(8,128)S(1)} copy-done((f32[256,512]{1,0:T(8,128)S(1)}, f32[256,512]{1,0:T(8,128)}, u32[]{:S(2)}) %copy-start.3) | copy-done | bytes 524312
  97.7 1.0 %shard_map.127 = (f32[512,512]{1,0:T(8,128)}, f32[512,512]{1,0:T(8,128)}) custom-call(s32[1]{0:T(128)} %bitcast.core_ref, bf16[16,32,512]{2,1,0:T(8,128)(2,1)S(1)} %all_to_all.17.matrix_ref), custom_call_target="tpu_custom_call" | custom-call | tf_op jit(solution)/shard_map/pallas_call | solution.py:53
  98.8 1.0 %shard_map.128 = (f32[512,512]{1,0:T(8,128)}, f32[512,512]{1,0:T(8,128)}) custom-call(s32[1]{0:T(128)} %bitcast.core_ref, bf16[16,32,512]{2,1,0:T(8,128)(2,1)S(1)} %collective-permute-done.10.matrix_ref, f32[512,512]{1,0:T(8,128)} %get-tuple-element.34.self_in, f32[512,512]{1,0:T(8,128)} %get-tuple-element.35.neigh_in), custom_call_target="tpu_custom_call", output_to_operand_aliasing={{0}: (2, {}), {1}: (3, {})} | custom-call | tf_op jit(solution)/shard_map/pallas_call | solution.py:53
  (30 shorter events, 5.2 us)
Async XLA Ops:
  0.6 10.2 %collective-permute-start = (bf16[256,512]{1,0:T(8,128)(2,1)}, bf16[256,512]{1,0:T(8,128)(2,1)S(1)}, u32[]{:S(2)}, u32[]{:S(2)}) collective-permute-start(bf16[256,512]{1,0:T(8,128)(2,1)} %refs_6_.1), channel_id=1, source_target_pairs={{0,2},{1,3},{2,4},{3,5},{4,6},{5,7},{6,8},{7,9},{8,10},{9,11},{10,... | collective-permute-start | bytes 786440 | tf_op jit(solution)/shard_map/ppermute | solution.py:21
  2.8 11.1 %collective-permute-start.1 = (bf16[256,512]{1,0:T(8,128)(2,1)}, bf16[256,512]{1,0:T(8,128)(2,1)S(1)}, u32[]{:S(2)}, u32[]{:S(2)}) collective-permute-start(bf16[256,512]{1,0:T(8,128)(2,1)} %refs_6_.1), channel_id=1, source_target_pairs={{0,30},{1,31},{2,0},{3,1},{4,2},{5,3},{6,4},{7,5},{8,6},{9,7},{10,... | collective-permute-start | bytes 786440 | tf_op jit(solution)/shard_map/ppermute | solution.py:21
  6.5 12.6 %collective-permute-start.2 = (bf16[256,512]{1,0:T(8,128)(2,1)}, bf16[256,512]{1,0:T(8,128)(2,1)S(1)}, u32[]{:S(2)}, u32[]{:S(2)}) collective-permute-start(bf16[256,512]{1,0:T(8,128)(2,1)} %refs_6_.1), channel_id=1, source_target_pairs={{0,1},{1,0},{2,3},{3,2},{4,5},{5,4},{6,7},{7,6},{8,9},{9,8},{10,11... | collective-permute-start | bytes 786440 | tf_op jit(solution)/shard_map/ppermute | solution.py:25
  10.8 8.4 %collective-permute-start.3 = (bf16[256,512]{1,0:T(8,128)(2,1)S(1)}, bf16[256,512]{1,0:T(8,128)(2,1)S(1)}, u32[]{:S(2)}, u32[]{:S(2)}) collective-permute-start(bf16[256,512]{1,0:T(8,128)(2,1)S(1)} %collective-permute-done.m2_ref), channel_id=1, source_target_pairs={{0,1},{1,0},{2,3},{3,2},{4,5},{5,4},{6,7},{7,6},{8,9},{9,8},{10,11... | collective-permute-start | bytes 786440 | tf_op jit(solution)/shard_map/ppermute | solution.py:25
  13.9 5.3 %collective-permute-start.4 = (bf16[256,512]{1,0:T(8,128)(2,1)S(1)}, bf16[256,512]{1,0:T(8,128)(2,1)S(1)}, u32[]{:S(2)}, u32[]{:S(2)}) collective-permute-start(bf16[256,512]{1,0:T(8,128)(2,1)S(1)} %collective-permute-done.1.p2_ref), channel_id=1, source_target_pairs={{0,1},{1,0},{2,3},{3,2},{4,5},{5,4},{6,7},{7,6},{8,9},{9,8},{10,11... | collective-permute-start | bytes 786440 | tf_op jit(solution)/shard_map/ppermute | solution.py:25
  13.9 0.7 copy-start.7
  13.9 0.7 copy-start.6
  14.0 0.7 copy-start.8
  14.0 0.7 copy-start.9
  14.7 1.2 %copy-start.2 = (bf16[2,16,128,128]{3,2,1,0:T(8,128)(2,1)S(1)}, bf16[2,16,128,128]{3,2,1,0:T(8,128)(2,1)}, u32[]{:S(2)}) copy-start(bf16[2,16,128,128]{3,2,1,0:T(8,128)(2,1)} %refs_3_.1) | copy-start | bytes 3145732
  15.9 0.9 copy-start.4
  16.8 0.9 copy-start.5
  17.8 1.4 %copy-start = (bf16[512,512]{1,0:T(8,128)(2,1)S(1)}, bf16[512,512]{1,0:T(8,128)(2,1)}, u32[]{:S(2)}) copy-start(bf16[512,512]{1,0:T(8,128)(2,1)} %ws_ref.3) | copy-start | bytes 1572868
  17.8 1.5 %copy-start.1 = (bf16[512,512]{1,0:T(8,128)(2,1)S(1)}, bf16[512,512]{1,0:T(8,128)(2,1)}, u32[]{:S(2)}) copy-start(bf16[512,512]{1,0:T(8,128)(2,1)} %wn_ref.3) | copy-start | bytes 1572868
  21.0 1.9 %collective-permute-start.9 = (bf16[2,256,512]{2,1,0:T(8,128)(2,1)S(1)}, bf16[2,256,512]{2,1,0:T(8,128)(2,1)S(1)}, u32[]{:S(2)}, u32[]{:S(2)}) collective-permute-start(bf16[2,256,512]{2,1,0:T(8,128)(2,1)S(1)} %get-tuple-element.27.mine_ref), channel_id=1, source_target_pairs={{0,1},{1,0},{2,3},{3,2},{4,5},{5,4},{6,7},{7,6},{8,9},{9,8},{10,11... | collective-permute-start | bytes 1572872 | tf_op jit(solution)/shard_map/ppermute | solution.py:25
  73.5 25.3 %collective-permute-start.10 = (bf16[16,32,512]{2,1,0:T(8,128)(2,1)S(1)}, bf16[16,32,512]{2,1,0:T(8,128)(2,1)S(1)}, u32[]{:S(2)}, u32[]{:S(2)}) collective-permute-start(bf16[16,32,512]{2,1,0:T(8,128)(2,1)S(1)} %all_to_all.17.matrix_ref), channel_id=1, source_target_pairs={{0,1},{1,0},{2,3},{3,2},{4,5},{5,4},{6,7},{7,6},{8,9},{9,8},{10,11... | collective-permute-start | bytes 1572872 | tf_op jit(solution)/shard_map/ppermute | solution.py:25
  79.6 8.1 %collective-permute-start.5 = (bf16[256,512]{1,0:T(8,128)(2,1)}, bf16[256,512]{1,0:T(8,128)(2,1)S(1)}, u32[]{:S(2)}, u32[]{:S(2)}) collective-permute-start(bf16[256,512]{1,0:T(8,128)(2,1)} %get-tuple-element.30), channel_id=1, source_target_pairs={{0,30},{1,31},{2,0},{3,1},{4,2},{5,3},{6,4},{7,5},{8,6},{9,7},{10,... | collective-permute-start | bytes 786440 | tf_op jit(solution)/shard_map/ppermute | solution.py:21
  80.5 10.4 %collective-permute-start.6 = (bf16[256,512]{1,0:T(8,128)(2,1)}, bf16[256,512]{1,0:T(8,128)(2,1)S(1)}, u32[]{:S(2)}, u32[]{:S(2)}) collective-permute-start(bf16[256,512]{1,0:T(8,128)(2,1)} %get-tuple-element.31), channel_id=1, source_target_pairs={{0,31},{1,0},{2,1},{3,2},{4,3},{5,4},{6,5},{7,6},{8,7},{9,8},{10,9... | collective-permute-start | bytes 786440 | tf_op jit(solution)/shard_map/ppermute | solution.py:21
  80.7 10.2 %collective-permute-start.7 = (bf16[256,512]{1,0:T(8,128)(2,1)}, bf16[256,512]{1,0:T(8,128)(2,1)S(1)}, u32[]{:S(2)}, u32[]{:S(2)}) collective-permute-start(bf16[256,512]{1,0:T(8,128)(2,1)} %get-tuple-element.32), channel_id=1, source_target_pairs={{0,1},{1,2},{2,3},{3,4},{4,5},{5,6},{6,7},{7,8},{8,9},{9,10},{10,1... | collective-permute-start | bytes 786440 | tf_op jit(solution)/shard_map/ppermute | solution.py:21
  82.2 13.6 %collective-permute-start.8 = (bf16[256,512]{1,0:T(8,128)(2,1)}, bf16[256,512]{1,0:T(8,128)(2,1)S(1)}, u32[]{:S(2)}, u32[]{:S(2)}) collective-permute-start(bf16[256,512]{1,0:T(8,128)(2,1)} %get-tuple-element.33), channel_id=1, source_target_pairs={{0,2},{1,3},{2,4},{3,5},{4,6},{5,7},{6,8},{7,9},{8,10},{9,11},{10,... | collective-permute-start | bytes 786440 | tf_op jit(solution)/shard_map/ppermute | solution.py:21
  95.8 1.0 %copy-start.3 = (f32[256,512]{1,0:T(8,128)S(1)}, f32[256,512]{1,0:T(8,128)}, u32[]{:S(2)}) copy-start(f32[256,512]{1,0:T(8,128)} %get-tuple-element.29.base_ref) | copy-start | bytes 1572868
